TPU v7x, 32 devices: a whole 2x2x4 slice. The times are simulated.
32 devices in a mesh: groups: 2 (over x), tm: 8 (over z, y), space: 2 (over core).
Axes of the slice: x: 2, y: 2, z: 4, core: 2. Of those that a mesh axis runs over, the one named last changes fastest.
Arguments:
- query_pre: bfloat16 [16, 8, 32, 2240], P(('groups', 'tm'), 'space'), parts along dimension 0, may hold values from -6 to 6
- key_pre: bfloat16 [16, 8, 32, 2240], P(('groups', 'tm'), 'space'), parts along dimension 0, may hold values from -6 to 6
- value_pre: bfloat16 [16, 8, 32, 2240], P(('groups', 'tm'), 'space'), parts along dimension 0, may hold values from -8 to 8
- grad_out: bfloat16 [16, 8, 32, 2240], P(('groups', 'tm'), 'space'), parts along dimension 0, may hold values from -96 to 96
- conv_taps: float32 [3, 3, 2240], replicated, may hold values from -4 to 4
Outputs:
- attended: bfloat16 [16, 8, 32, 2240], P(('groups', 'tm'), 'space'), parts along dimension 0
- query_grad: bfloat16 [16, 8, 32, 2240], P(('groups', 'tm'), 'space'), parts along dimension 0
- key_grad: bfloat16 [16, 8, 32, 2240], P(('groups', 'tm'), 'space'), parts along dimension 0
- value_grad: bfloat16 [16, 8, 32, 2240], P(('groups', 'tm'), 'space'), parts along dimension 0
- taps_grad: float32 [6, 3, 2240], P('groups'), parts along dimension 0
There are 2 independent parts, one for each index of `groups`. A program takes and returns all parts, laid end to end along the dimension named above; an argument that names none is the same for every part. Nothing has to cross between parts.
All inputs are finite; a program needn't handle non-finite values.
Results may differ from a plain program's by a relative error of at most 0.013.
Values may be sent and summed in bfloat16 or wider, within the bound.
A program may use at most 128 MiB of HBM per device.

v0:
```python
import jax
import jax.numpy as jnp
from jax import lax
from jax.sharding import PartitionSpec as P

HEADS = 20
HEAD_DIM = 112


def extended(block, sides, width):
    for axis, dim in sides:
        count = lax.axis_size(axis)
        forward = [(i, i + 1) for i in range(count - 1)]
        backward = [(target, source) for source, target in forward]
        low = lax.ppermute(
            lax.slice_in_dim(block, block.shape[dim] - width, None, axis=dim), axis, forward
        )
        high = lax.ppermute(lax.slice_in_dim(block, 0, width, axis=dim), axis, backward)
        block = jnp.concatenate([low, block, high], axis=dim)
    return block


def carried_in(part, axis, combine, identity):
    place = lax.axis_index(axis)
    gathered = jax.tree.map(lambda a: lax.all_gather(a, axis), part)
    state = jax.tree.map(lambda a, e: jnp.zeros_like(a) + jnp.asarray(e, a.dtype), part, identity)

    def one(turn, state):
        return combine(
            state, jax.tree.map(lambda a: lax.dynamic_index_in_dim(a, turn, 0, False), gathered)
        )

    return lax.fori_loop(0, place, one, state)


def carried_in_2(x, axis, join, neutral):
    count = lax.axis_size(axis)
    place = lax.axis_index(axis)
    ahead = count - 1 - place
    gathered = jax.tree.map(
        lambda a, kind: lax.all_gather(a.astype(kind), axis), x, (jnp.bfloat16, jnp.bfloat16)
    )
    state = jax.tree.map(lambda a, e: jnp.zeros_like(a) + jnp.asarray(e, a.dtype), x, neutral)

    def one(turn, state):
        source = count - 1 - turn
        return join(
            state,
            jax.tree.map(
                lambda a, own: lax.dynamic_index_in_dim(a, source, 0, False).astype(own.dtype),
                gathered,
                x,
            ),
        )

    return lax.fori_loop(0, ahead, one, state)


def mix_rows(padded, conv_taps, row_count, col_count, flipped):
    summed = jnp.zeros(padded.shape[:1] + (row_count, col_count, padded.shape[3]), jnp.float32)
    for row_off in range(3):
        for col_off in range(3):
            if flipped:
                window = padded[
                    :, 2 - row_off : 2 - row_off + row_count, 2 - col_off : 2 - col_off + col_count
                ]
            else:
                window = padded[:, row_off : row_off + row_count, col_off : col_off + col_count]
            summed = summed + conv_taps[row_off, col_off] * window
    return summed


def add_pair(earlier, later):
    return (earlier[0] + later[0], earlier[1] + later[1])


def shards(query_pre, key_pre, value_pre, grad_out, conv_taps):
    frame_count, row_count, col_count, model_width = value_pre.shape
    head_count = HEADS
    head_size = HEAD_DIM
    token_count = frame_count * row_count * col_count
    split = (token_count, head_count, head_size)
    highest = lax.Precision.HIGHEST
    value_rows, grad_band = (
        extended(value_pre, (("space", 1),), 1),
        extended(grad_out, (("space", 1),), 1),
    )
    value_pad = jnp.pad(value_rows, ((0, 0), (0, 0), (1, 1), (0, 0)))
    local = mix_rows(value_pad, conv_taps, row_count, col_count, False)
    queries = jnp.maximum(query_pre, 0).reshape(split)
    keys = jnp.maximum(key_pre, 0).reshape(split)
    values = value_pre.reshape(split)
    partial_value = jnp.einsum("the,thd->hed", keys, values, preferred_element_type=jnp.float32)
    key_sum = jnp.sum(keys, axis=0, dtype=jnp.float32)
    half_state, half_sum = (
        lax.psum_scatter(partial_value, "space", scatter_dimension=0, tiled=True),
        lax.psum_scatter(key_sum, "space", scatter_dimension=0, tiled=True),
    )
    before = carried_in(
        (half_state, half_sum),
        "tm",
        add_pair,
        (jnp.zeros_like(half_state), jnp.zeros_like(half_sum)),
    )
    kv_state, key_total = (
        lax.all_gather(before[0] + half_state, "space", axis=0, tiled=True),
        lax.all_gather(before[1] + half_sum, "space", axis=0, tiled=True),
    )
    query_f32 = queries.astype(jnp.float32)
    numerator = jnp.einsum("the,hed->thd", query_f32, kv_state, precision=highest)
    denominator = jnp.einsum("the,he->th", query_f32, key_total, precision=highest) + 1.0
    output_f32 = numerator / denominator[..., None]
    attended = (output_f32.reshape(value_pre.shape) + local).astype(jnp.bfloat16)
    cotangent = grad_out.astype(jnp.float32).reshape(split)
    grad_num = cotangent / denominator[..., None]
    grad_den = -jnp.sum(cotangent * output_f32, axis=-1) / denominator
    grad_query = (
        jnp.einsum("thd,hed->the", grad_num, kv_state, precision=highest)
        + grad_den[..., None] * key_total[None]
    )
    grad_partial = jnp.einsum("the,thd->hed", query_f32, grad_num, precision=highest)
    grad_keysum = jnp.einsum("th,the->he", grad_den, query_f32, precision=highest)
    half_grad, half_keysum = (
        lax.psum_scatter(grad_partial, "space", scatter_dimension=0, tiled=True),
        lax.psum_scatter(grad_keysum, "space", scatter_dimension=0, tiled=True),
    )
    after = carried_in_2(
        (half_grad, half_keysum),
        "tm",
        add_pair,
        (jnp.zeros_like(half_grad), jnp.zeros_like(half_keysum)),
    )
    grad_state, grad_total = (
        lax.all_gather(
            (after[0] + half_grad).astype(jnp.bfloat16), "space", axis=0, tiled=True
        ).astype(jnp.float32),
        lax.all_gather(
            (after[1] + half_keysum).astype(jnp.bfloat16), "space", axis=0, tiled=True
        ).astype(jnp.float32),
    )
    grad_key = (
        jnp.einsum("thd,hed->the", values.astype(jnp.float32), grad_state, precision=highest)
        + grad_total[None]
    )
    grad_mixed = jnp.einsum(
        "the,hed->thd", keys.astype(jnp.float32), grad_state, precision=highest
    ).reshape(value_pre.shape)
    query_grad = jnp.where(query_pre > 0, grad_query.reshape(value_pre.shape), 0.0).astype(
        jnp.bfloat16
    )
    key_grad = jnp.where(key_pre > 0, grad_key.reshape(value_pre.shape), 0.0).astype(jnp.bfloat16)
    grad_pad = jnp.pad(grad_band, ((0, 0), (0, 0), (1, 1), (0, 0)))
    value_grad = (grad_mixed + mix_rows(grad_pad, conv_taps, row_count, col_count, True)).astype(
        jnp.bfloat16
    )
    cotangent_full = grad_out.astype(jnp.float32)
    tap_rows = []
    for row_off in range(3):
        tap_cols = []
        for col_off in range(3):
            window = value_pad[:, row_off : row_off + row_count, col_off : col_off + col_count]
            tap_cols.append(jnp.sum(cotangent_full * window, axis=(0, 1, 2)))
        tap_rows.append(jnp.stack(tap_cols))
    taps_grad = lax.psum(jnp.stack(tap_rows), ("tm", "space"))
    return (attended, query_grad, key_grad, value_grad, taps_grad)


def solution(mesh):
    return jax.shard_map(
        shards,
        mesh=mesh,
        in_specs=(
            P(("groups", "tm"), "space", None, None),
            P(("groups", "tm"), "space", None, None),
            P(("groups", "tm"), "space", None, None),
            P(("groups", "tm"), "space", None, None),
            P(),
        ),
        out_specs=(
            P(("groups", "tm"), "space", None, None),
            P(("groups", "tm"), "space", None, None),
            P(("groups", "tm"), "space", None, None),
            P(("groups", "tm"), "space", None, None),
            P("groups", None, None),
        ),
        check_vma=False,
    )
```

profile of v0, /device:TPU:0, one launch (start us, length us, event | category | flops | bytes accessed | tf_op | source)
XLA Modules:
  0.0 252.8 jit_solution(9472925568814212947)
XLA Ops:
  11.8 1.5 fusion.43
  13.3 11.3 %reduce-scatter.7.cloned.1.call-done = f32[10,112,112]{2,1,0:T(8,128)} async-done(((f32[20,112,112]{2,1,0:T(8,128)}), f32[10,112,112]{2,1,0:T(8,128)}) %reduce-scatter.7.cloned.1.call-update) | async-done | bytes 501776 | tf_op jit(solution)/shard_map/reduce_scatter | solution.py:96
  24.9 2.8 %fusion = f32[16,112]{1,0:T(8,128)S(1)} fusion(f32[20,112]{1,0:T(8,128)S(1)} %reduce_sum.102), kind=kCustom, calls=%all-reduce-scatter | all-reduce-scatter fusion | flops 3585 | bytes 16640
  27.8 2.1 collective-permute-start.4
  34.2 2.0 reshape.72
  36.9 31.9 %all-gather.4 = f32[8,10,112]{2,1,0:T(8,128)S(1)} all-gather(f32[1,10,112]{2,1,0:T(8,128)S(1)} %fusion.37), channel_id=3, replica_groups=mesh['groups'=2,'tm'=8,'space'=2] {'tm'}, dimensions={0}, use_global_device_ids=true | all-gather | bytes 40320 | tf_op jit(solution)/shard_map/all_gather | solution.py:25
  68.8 37.5 %all-gather.11.cloned.1.call-done = f32[80,112,112]{2,1,0:T(8,128)} async-done(((f32[10,112,112]{2,1,0:T(8,128)}), f32[80,112,112]{2,1,0:T(8,128)}) %all-gather.11.cloned.1.call-update) | async-done | bytes 4014096 | tf_op jit(solution)/shard_map/all_gather | solution.py:25
  107.2 1.8 all-gather.5
  109.6 2.4 fusion.33
  112.0 15.5 %reduce-scatter.9.cloned.1.call-done = f32[10,112,112]{2,1,0:T(8,128)} async-done(((f32[20,112,112]{2,1,0:T(8,128)}), f32[10,112,112]{2,1,0:T(8,128)}) %reduce-scatter.9.cloned.1.call-update) | async-done | bytes 501776 | tf_op jit(solution)/shard_map/reduce_scatter | solution.py:124
  127.6 1.8 convert_element_type.134
  130.8 3.0 %collective-permute-start = (bf16[1,1,32,2240]{3,2,1,0:T(8,128)(2,1)S(1)}, bf16[1,1,32,2240]{3,2,1,0:T(8,128)(2,1)S(1)}, u32[]{:S(2)}, u32[]{:S(2)}) collective-permute-start(bf16[1,1,32,2240]{3,2,1,0:T(8,128)(2,1)S(1)} %get-tuple-element.171), channel_id=1, source_target_pairs={{0,1},{2,3},{4,5},{6,7},{8,9},{10,11},{12,13},{14,15},{16,17},{18,... | collective-permute-start | bytes 430088 | tf_op jit(solution)/shard_map/ppermute | solution.py:15
  135.8 3.7 %collective-permute-start.2 = (bf16[1,1,32,2240]{3,2,1,0:T(8,128)(2,1)}, bf16[1,1,32,2240]{3,2,1,0:T(8,128)(2,1)}, u32[]{:S(2)}, u32[]{:S(2)}) collective-permute-start(bf16[1,1,32,2240]{3,2,1,0:T(8,128)(2,1)} %get-tuple-element.169), channel_id=1, source_target_pairs={{0,1},{2,3},{4,5},{6,7},{8,9},{10,11},{12,13},{14,15},{16,17},{18,... | collective-permute-start | bytes 430088 | tf_op jit(solution)/shard_map/ppermute | solution.py:15
  143.5 1.5 select_maximum_fusion
  146.7 2.9 %all_gather.40 = f32[20,112,112]{2,1,0:T(8,128)S(1)} all-gather(f32[10,112,112]{2,1,0:T(8,128)S(1)} %add.145), channel_id=1, replica_groups=mesh['groups'=2,'tm'=8,'space'=2] {'space'}, dimensions={0}, use_global_device_ids=true | all-gather | bytes 1505280 | tf_op jit(solution)/shard_map/all_gather | solution.py:106
  149.7 2.7 %multiply_reduce_fusion = (f32[128,20]{0,1:T(8,128)}, f32[128,20,112]{0,2,1:T(8,128)}) fusion(f32[128,20,112]{0,2,1:T(8,128)S(1)} %copy-done.18, f32[128,20]{0,1:T(8,128)S(1)} %copy-done.37, f32[20,112,112]{2,1,0:T(8,128)S(1)} %all_gather.40, bf16[128,20,112]{0,2,1:T(8,128)(2,1)S(1)} %copy-done.10), kind=kOutput, calls=%fused_computation.62 | convolution fusion | flops 386209280 | bytes 3891200 | tf_op jit(solution)/shard_map/the,hed->thd/dot_general | solution.py:110
  152.4 2.9 %copy.41 = f32[128,20,112]{2,1,0:T(8,128)} copy(f32[128,20,112]{0,2,1:T(8,128)} %get-tuple-element.174) | data formatting | bytes 2293760 | tf_op jit(solution)/shard_map/div | solution.py:112
  155.3 2.7 %reshape.73 = f32[1,4,32,2240]{3,2,1,0:T(8,128)} reshape(f32[128,20,112]{2,1,0:T(8,128)} %copy.41) | data formatting | bytes 2293760 | tf_op jit(solution)/shard_map/reshape | solution.py:113
  159.8 2.7 %fusion.1 = f32[16,112]{1,0:T(8,128)S(1)} fusion(f32[20,112]{1,0:T(8,128)S(1)} %bitcast.88), kind=kCustom, calls=%all-reduce-scatter.1 | all-reduce-scatter fusion | flops 3585 | bytes 16640
  162.4 2.2 collective-permute-start.5
  164.8 3.3 %fusion.15 = bf16[1,4,32,2240]{3,2,1,0:T(8,128)(2,1)} fusion(f32[1,4,32,2240]{3,2,1,0:T(8,128)} %reshape.73, bf16[1,4,32,2240]{3,2,1,0:T(8,128)(2,1)S(1)} %copy-done, bf16[1,1,32,2240]{3,2,1,0:T(8,128)(2,1)S(1)} %collective-permute-done.1, bf16[1,1,32,2240]{3,2,1,0:T(8,128)(2,1)} %copy-done.14, f32[2240]{0:T(1024)} %get-tuple-element.143, ...), kind=kLoop, calls=%fused_computation.42 | loop fusion | flops 8601600 | bytes 6101760 | tf_op jit(solution)/shard_map/convert_element_type | solution.py:113
  171.5 31.1 %all-gather.6 = bf16[8,10,112]{2,1,0:T(8,128)(2,1)S(1)} all-gather(bf16[1,10,112]{2,1,0:T(8,128)(2,1)S(1)} %fusion.39), channel_id=5, replica_groups=mesh['groups'=2,'tm'=8,'space'=2] {'tm'}, dimensions={0}, use_global_device_ids=true | all-gather | bytes 20160 | tf_op jit(solution)/shard_map/all_gather | solution.py:41
  202.7 7.8 %while.27 = (s32[]{:T(128)}, f32[10,112,112]{2,1,0:T(8,128)S(1)}, f32[10,112]{1,0:T(8,128)S(1)}, s32[]{:T(128)}, bf16[8,10,112,112]{3,2,1,0:T(8,128)(2,1)}, /*in...) while((s32[]{:T(128)}, f32[10,112,112]{2,1,0:T(8,128)S(1)}, ...), condition=%wide.region_9.10_spmd, body=%wide.region_8.9_spmd.sunk | while | flops 253126 | bytes 1265763 | solution.py:56
  210.6 2.3 all_gather.46
  213.0 1.9 all-gather.7
  217.6 1.6 copy.47
  220.6 1.6 copy.50
  222.2 1.9 reshape.77
  224.2 2.8 %select_convert_fusion = (bf16[1,4,32,2240]{3,2,1,0:T(8,128)(2,1)}, bf16[1,4,32,2240]{3,2,1,0:T(8,128)(2,1)}) fusion(bf16[1,4,32,2240]{3,2,1,0:T(8,128)(2,1)} %reshape.76, bf16[1,4,32,2240]{3,2,1,0:T(8,128)(2,1)S(1)} %copy-done.4, bf16[1,4,32,2240]{3,2,1,0:T(8,128)(2,1)} %reshape.75, bf16[1,4,32,2240]{3,2,1,0:T(8,128)(2,1)} %param.9), kind=kLoop, calls=%fused_computation.59 | loop fusion | flops 2007040 | bytes 3440640 | tf_op jit(solution)/shard_map/convert_element_type | solution.py:151
  227.1 2.7 %fusion.22 = bf16[1,4,32,2240]{3,2,1,0:T(8,128)(2,1)} fusion(f32[1,4,32,2240]{3,2,1,0:T(8,128)S(1)} %reshape.77, bf16[1,4,32,2240]{3,2,1,0:T(8,128)(2,1)S(1)} %copy-done.2, bf16[1,6,34,2240]{3,2,1,0:T(8,128)(2,1)S(1)} %select_maximum_fusion, bf16[1,1,32,2240]{3,2,1,0:T(8,128)(2,1)} %collective-permute-done.2, bf16[1,1,32,2240]{3,2,1,0:T(8,128)(2,1)S(1)} %copy-done.21, ...), kind=kLoop, calls=%fused_computation.49 | loop fusion | flops 8601600 | bytes 6101760 | tf_op jit(solution)/shard_map/convert_element_type | solution.py:153
  229.8 14.3 %all-reduce.8.cloned.1.call-done = f32[3,3,2240]{2,1,0:T(4,128)} async-done(((f32[3,3,2240]{2,1,0:T(4,128)}), f32[3,3,2240]{2,1,0:T(4,128)}) %all-reduce.8.cloned.1.call-update) | async-done | bytes 80656 | tf_op jit(solution)/shard_map/psum | solution.py:164
  244.2 1.6 copy.83
  (171 shorter events, 35.8 us)
Async XLA Ops:
  8.0 16.6 %reduce-scatter.7.cloned.1.call-start = ((), (), s32[]{:S(2)}) async-start(), calls=%async_computation.2 | async-start | bytes 1720320 | tf_op jit(solution)/shard_map/reduce_scatter | solution.py:96
  13.3 11.4 %copy-start.3 = (bf16[1,4,32,2240]{3,2,1,0:T(8,128)(2,1)S(1)}, bf16[1,4,32,2240]{3,2,1,0:T(8,128)(2,1)}, u32[]{:S(2)}) copy-start(bf16[1,4,32,2240]{3,2,1,0:T(8,128)(2,1)} %param.10) | copy-start | bytes 1720324
  13.3 16.6 %copy-start.12 = (bf16[1,4,32,2240]{3,2,1,0:T(8,128)(2,1)S(1)}, bf16[1,4,32,2240]{3,2,1,0:T(8,128)(2,1)}, u32[]{:S(2)}) copy-start(bf16[1,4,32,2240]{3,2,1,0:T(8,128)(2,1)} %param.9) | copy-start | bytes 1720324
  13.3 93.0 %all-gather.11.cloned.1.call-start = ((), (), s32[]{:S(2)}) async-start(), calls=%async_computation.5 | async-start | bytes 5160960 | tf_op jit(solution)/shard_map/all_gather | solution.py:25
  24.6 6.1 %copy-start.1 = (bf16[1,4,32,2240]{3,2,1,0:T(8,128)(2,1)S(1)}, bf16[1,4,32,2240]{3,2,1,0:T(8,128)(2,1)}, u32[]{:S(2)}) copy-start(bf16[1,4,32,2240]{3,2,1,0:T(8,128)(2,1)} %param.12) | copy-start | bytes 1720324
  24.6 102.9 %reduce-scatter.9.cloned.1.call-start = ((), (), s32[]{:S(2)}) async-start(), calls=%async_computation.3 | async-start | bytes 1720320 | tf_op jit(solution)/shard_map/reduce_scatter | solution.py:124
  27.8 8.9 %collective-permute-start.4 = (f32[6,112]{1,0:T(8,128)S(1)}, f32[6,112]{1,0:T(8,128)S(1)}, u32[]{:S(2)}, u32[]{:S(2)}) collective-permute-start(f32[6,112]{1,0:T(8,128)S(1)} %slice.158), channel_id=1, source_target_pairs={{0,1},{2,3},{4,5},{6,7},{8,9},{10,11},{12,13},{14,15},{16,17},{18,... | collective-permute-start | bytes 8072
  36.7 72.9 %copy-start.9 = (bf16[128,20,112]{0,2,1:T(8,128)(2,1)}, bf16[128,20,112]{0,2,1:T(8,128)(2,1)S(1)}, u32[]{:S(2)}) copy-start(bf16[128,20,112]{0,2,1:T(8,128)(2,1)S(1)} %copy.40) | copy-start | bytes 1720324
  36.8 69.4 %copy-start.31 = (f32[22,112]{1,0:T(8,128)}, f32[22,112]{1,0:T(8,128)S(1)}, u32[]{:S(2)}) copy-start(f32[22,112]{1,0:T(8,128)S(1)} %concatenate.24) | copy-start | bytes 29572
  106.3 3.2 %copy-start.17 = (f32[128,20,112]{0,2,1:T(8,128)S(1)}, f32[128,20,112]{0,2,1:T(8,128)}, u32[]{:S(2)}) copy-start(f32[128,20,112]{0,2,1:T(8,128)} %copy.42) | copy-start | bytes 3440644
  112.0 27.6 %copy-start.32 = (f32[3,3,2240]{2,1,0:T(4,128)S(1)}, f32[3,3,2240]{2,1,0:T(4,128)}, u32[]{:S(2)}) copy-start(f32[3,3,2240]{2,1,0:T(4,128)} %param.13) | copy-start | bytes 241924
  112.0 90.7 %all-gather.13.cloned.1.call-start = ((), (), s32[]{:S(2)}) async-start(), calls=%async_computation.6 | async-start | bytes 2580480 | tf_op jit(solution)/shard_map/all_gather | solution.py:41
  129.4 114.8 %all-reduce.8.cloned.1.call-start = ((), (), s32[]{:S(2)}) async-start(), calls=%async_computation.4 | async-start | bytes 221184 | tf_op jit(solution)/shard_map/psum | solution.py:164
  129.5 10.9 %collective-permute-start.1 = (bf16[1,1,32,2240]{3,2,1,0:T(8,128)(2,1)S(1)}, bf16[1,1,32,2240]{3,2,1,0:T(8,128)(2,1)S(1)}, u32[]{:S(2)}, u32[]{:S(2)}) collective-permute-start(bf16[1,1,32,2240]{3,2,1,0:T(8,128)(2,1)S(1)} %get-tuple-element.172), channel_id=1, source_target_pairs={{1,0},{3,2},{5,4},{7,6},{9,8},{11,10},{13,12},{15,14},{17,16},{19,... | collective-permute-start | bytes 430088 | tf_op jit(solution)/shard_map/ppermute | solution.py:18
  130.8 9.6 %collective-permute-start = (bf16[1,1,32,2240]{3,2,1,0:T(8,128)(2,1)S(1)}, bf16[1,1,32,2240]{3,2,1,0:T(8,128)(2,1)S(1)}, u32[]{:S(2)}, u32[]{:S(2)}) collective-permute-start(bf16[1,1,32,2240]{3,2,1,0:T(8,128)(2,1)S(1)} %get-tuple-element.171), channel_id=1, source_target_pairs={{0,1},{2,3},{4,5},{6,7},{8,9},{10,11},{12,13},{14,15},{16,17},{18,... | collective-permute-start | bytes 430088 | tf_op jit(solution)/shard_map/ppermute | solution.py:15
  134.6 8.2 %collective-permute-start.3 = (bf16[1,1,32,2240]{3,2,1,0:T(8,128)(2,1)}, bf16[1,1,32,2240]{3,2,1,0:T(8,128)(2,1)S(1)}, u32[]{:S(2)}, u32[]{:S(2)}) collective-permute-start(bf16[1,1,32,2240]{3,2,1,0:T(8,128)(2,1)} %get-tuple-element.170), channel_id=1, source_target_pairs={{1,0},{3,2},{5,4},{7,6},{9,8},{11,10},{13,12},{15,14},{17,16},{19,... | collective-permute-start | bytes 430088 | tf_op jit(solution)/shard_map/ppermute | solution.py:18
  135.8 7.6 %collective-permute-start.2 = (bf16[1,1,32,2240]{3,2,1,0:T(8,128)(2,1)}, bf16[1,1,32,2240]{3,2,1,0:T(8,128)(2,1)}, u32[]{:S(2)}, u32[]{:S(2)}) collective-permute-start(bf16[1,1,32,2240]{3,2,1,0:T(8,128)(2,1)} %get-tuple-element.169), channel_id=1, source_target_pairs={{0,1},{2,3},{4,5},{6,7},{8,9},{10,11},{12,13},{14,15},{16,17},{18,... | collective-permute-start | bytes 430088 | tf_op jit(solution)/shard_map/ppermute | solution.py:15
  145.6 4.1 %copy-start.37 = (f32[128,20]{0,1:T(8,128)S(1)}, f32[128,20]{0,1:T(8,128)}, u32[]{:S(2)}) copy-start(f32[128,20]{0,1:T(8,128)} %copy-done.36) | copy-start | bytes 30724
  146.7 3.0 %copy-start.10 = (bf16[128,20,112]{0,2,1:T(8,128)(2,1)S(1)}, bf16[128,20,112]{0,2,1:T(8,128)(2,1)}, u32[]{:S(2)}) copy-start(bf16[128,20,112]{0,2,1:T(8,128)(2,1)} %copy-done.9) | copy-start | bytes 1720324
  146.7 3.0 %copy-start.18 = (f32[128,20,112]{0,2,1:T(8,128)S(1)}, f32[128,20,112]{0,2,1:T(8,128)}, u32[]{:S(2)}) copy-start(f32[128,20,112]{0,2,1:T(8,128)} %copy.42) | copy-start | bytes 3440644
  155.3 9.4 %copy-start.22 = (f32[2240]{0:T(1024)S(1)}, f32[2240]{0:T(1024)}, u32[]{:S(2)}) copy-start(f32[2240]{0:T(1024)} %get-tuple-element.137) | copy-start | bytes 26884
  162.4 8.9 %collective-permute-start.5 = (f32[6,112]{1,0:T(8,128)S(1)}, f32[6,112]{1,0:T(8,128)S(1)}, u32[]{:S(2)}, u32[]{:S(2)}) collective-permute-start(f32[6,112]{1,0:T(8,128)S(1)} %slice.159), channel_id=1, source_target_pairs={{0,1},{2,3},{4,5},{6,7},{8,9},{10,11},{12,13},{14,15},{16,17},{18,... | collective-permute-start | bytes 8072
  164.7 3.4 %copy-start.16 = (f32[20,112,112]{2,1,0:T(8,128)S(1)}, f32[20,112,112]{2,1,0:T(8,128)}, u32[]{:S(2)}) copy-start(f32[20,112,112]{2,1,0:T(8,128)} %copy-done.15) | copy-start | bytes 3010564
  164.7 3.4 %copy-start.19 = (f32[128,20,112]{0,2,1:T(8,128)S(1)}, f32[128,20,112]{0,2,1:T(8,128)}, u32[]{:S(2)}) copy-start(f32[128,20,112]{0,2,1:T(8,128)} %copy.42) | copy-start | bytes 3440644
  164.7 3.4 %copy-start.34 = (f32[128,20]{0,1:T(8,128)S(1)}, f32[128,20]{0,1:T(8,128)}, u32[]{:S(2)}) copy-start(f32[128,20]{0,1:T(8,128)} %copy-done.33) | copy-start | bytes 30724
  164.7 3.4 %copy-start.35 = (f32[20,112]{1,0:T(8,128)S(1)}, f32[20,112]{1,0:T(8,128)}, u32[]{:S(2)}) copy-start(f32[20,112]{1,0:T(8,128)} %reshape.87) | copy-start | bytes 26884
  164.7 3.4 %copy-start.38 = (f32[128,20]{0,1:T(8,128)S(1)}, f32[128,20]{0,1:T(8,128)}, u32[]{:S(2)}) copy-start(f32[128,20]{0,1:T(8,128)} %copy-done.36) | copy-start | bytes 30724
  202.7 7.8 %copy-start.13 = (f32[10,112,112]{2,1,0:T(8,128)S(1)}, f32[10,112,112]{2,1,0:T(8,128)}, u32[]{:S(2)}) copy-start(f32[10,112,112]{2,1,0:T(8,128)} %reduce-scatter.9.cloned.1.call-done) | copy-start | bytes 1505284
  210.5 4.4 %copy-start.6 = (bf16[128,20,112]{0,2,1:T(8,128)(2,1)S(1)}, bf16[128,20,112]{0,2,1:T(8,128)(2,1)}, u32[]{:S(2)}) copy-start(bf16[128,20,112]{0,2,1:T(8,128)(2,1)} %copy-done.5) | copy-start | bytes 1720324
  213.0 3.4 %copy-start.8 = (bf16[128,20,112]{0,2,1:T(8,128)(2,1)S(1)}, bf16[128,20,112]{0,2,1:T(8,128)(2,1)}, u32[]{:S(2)}) copy-start(bf16[128,20,112]{0,2,1:T(8,128)(2,1)} %copy-done.7) | copy-start | bytes 1720324
  217.6 3.0 %copy-start.11 = (f32[128,20,112]{0,2,1:T(8,128)S(1)}, f32[128,20,112]{0,2,1:T(8,128)}, u32[]{:S(2)}) copy-start(f32[128,20,112]{0,2,1:T(8,128)} %convolution_bitcast_fusion) | copy-start | bytes 3440644
  224.1 2.9 %copy-start.2 = (bf16[1,4,32,2240]{3,2,1,0:T(8,128)(2,1)S(1)}, bf16[1,4,32,2240]{3,2,1,0:T(8,128)(2,1)}, u32[]{:S(2)}) copy-start(bf16[1,4,32,2240]{3,2,1,0:T(8,128)(2,1)} %param.12) | copy-start | bytes 1720324
  (19 other events, 41.5 us)
Sparse Core Ops, SparseCore 0:
  13.4 11.1 reduce-scatter.6
  26.8 79.4 all-gather.10
  112.1 15.4 reduce-scatter.8
  129.6 52.6 all-gather.12
Sparse Core Ops, SparseCore 1:
  142.9 101.2 all-reduce.7
where the time goes:
time: 256 us; the launch traced here: 253 us
  waiting for transfers between devices  78.7 us (31%)
  blocking collectives  77.6 us (30%)
  other arithmetic  26.9 us (11%)
  local copies, waits for them, and re-layouts  26.9 us (11%)
  between operations  16.6 us (6%)
  starting transfers between devices  13.8 us (5%)
  matrix products  12.1 us (5%)
    all_gather x1, waiting for transfers between devices, carried_in(): gathered = jax.tree.map(lambda a: lax.all_gather(a, axis), part)  37.5 us
    all_gather x1, blocking collectives, carried_in(): gathered = jax.tree.map(lambda a: lax.all_gather(a, axis), part)  31.9 us
    all_gather x1, blocking collectives, carried_in_2(): lax.all_gather(a.astype(kind), axis)  31.1 us
    reduce_scatter x1, waiting for transfers between devices, shards(): lax.psum_scatter(grad_partial, 'space', scatter_dimension=0, tiled=True)  15.5 us
    psum x1, waiting for transfers between devices, shards(): taps_grad = lax.psum(jnp.stack(tap_rows), ('tm', 'space'))  14.3 us
    reduce_scatter x1, waiting for transfers between devices, shards(): lax.psum_scatter(partial_value, 'space', scatter_dimension=0, tiled=True)  11.3 us
    add x14, other arithmetic, add_pair(): return (earlier[0] + later[0], earlier[1] + later[1])  7.59 us
    ppermute x2, starting transfers between devices, extended(): lax.ppermute(lax.slice_in_dim(block, block.shape[dim] - width, None, axis...  6.74 us
  transfers between devices with their start and end apart: 11, of which 4 were waited for; matrix products, arithmetic and copies ran while one was open for 23% of the time, Pallas kernels for 0%

commit v1 on v0

v1 whole, which is shorter than its diff:
```python
import jax
import jax.numpy as jnp
from jax import lax
from jax.experimental import pallas as pl
from jax.experimental.pallas import tpu as pltpu
from jax.sharding import PartitionSpec as P

HEADS = 20
HEAD_DIM = 112
LANES = 128
F32 = jnp.float32
BF16 = jnp.bfloat16
VMEM_LIMIT = 60 * 1024 * 1024


def call(body, out_shape, *args):
    return pl.pallas_call(
        body,
        out_shape=out_shape,
        in_specs=[pl.BlockSpec(memory_space=pltpu.VMEM)] * len(args),
        out_specs=jax.tree.map(lambda _: pl.BlockSpec(memory_space=pltpu.VMEM), out_shape),
        compiler_params=pltpu.CompilerParams(vmem_limit_bytes=VMEM_LIMIT),
    )(*args)


def struct(shape, dtype):
    return jax.ShapeDtypeStruct(shape, dtype)


def dot(a, b, dims):
    return lax.dot_general(a, b, (dims, ((), ())), preferred_element_type=F32)


def high_low(x):
    high = x.astype(BF16).astype(F32)
    return high, x - high


def conv_body(rows, cols, value_ref, grad_ref, taps_ref, local_ref, conv_ref, taps_grad_ref):
    width = value_ref.shape[1]
    count = rows * cols
    for low in range(0, width, LANES):
        lanes = slice(low, min(low + LANES, width))
        value = value_ref[:, lanes].astype(F32)
        grad = grad_ref[:, lanes].astype(F32)
        col = lax.broadcasted_iota(jnp.int32, value.shape, 0) % cols
        total = value.shape[0]

        def left(x):
            return jnp.where(col == 0, 0.0, pltpu.roll(x, 1, 0))

        def right(x):
            return jnp.where(col == cols - 1, 0.0, pltpu.roll(x, total - 1, 0))

        values = (left(value), value, right(value))
        grads = (right(grad), grad, left(grad))
        centre = grad[cols : cols + count]
        local = conv = None
        for a in range(3):
            for b in range(3):
                tap = taps_ref[3 * a + b : 3 * a + b + 1, lanes]
                window = values[b][a * cols : a * cols + count]
                back = grads[b][(2 - a) * cols : (2 - a) * cols + count]
                local = tap * window if local is None else local + tap * window
                conv = tap * back if conv is None else conv + tap * back
                taps_grad_ref[3 * a + b : 3 * a + b + 1, lanes] = jnp.sum(
                    centre * window, axis=0, keepdims=True
                )
        local_ref[:, lanes] = local
        conv_ref[:, lanes] = conv


def guarded(x):
    return jnp.where(x > 0, 1.0 / jnp.where(x > 0, x, 1.0), 0.0)


def partial_body(key_ref, value_ref, out_ref):
    size = HEAD_DIM
    count = key_ref.shape[0]
    ones = jnp.where(
        lax.broadcasted_iota(jnp.int32, (count, LANES - size), 1) == 0, 1.0, 0.0
    ).astype(BF16)
    lane = lax.broadcasted_iota(jnp.int32, (size, LANES), 1)
    lane_row = lax.broadcasted_iota(jnp.int32, (1, LANES), 1)
    extra = lax.broadcasted_iota(jnp.int32, (LANES - size, LANES), 0)
    pad = jnp.zeros((1, LANES - size), F32)
    for head in range(HEADS):
        lanes = slice(head * size, (head + 1) * size)
        key = jnp.maximum(key_ref[:, lanes], 0)
        value = jnp.concatenate([value_ref[:, lanes], ones], axis=1)
        sums = dot(key, value, ((0,), (0,)))
        keys = sums[:, size : size + 1]
        inverse = guarded(jnp.sum(keys, axis=0, keepdims=True))
        mean = jnp.where(lane_row < size, jnp.sum(sums, axis=0, keepdims=True) * inverse, 0.0)
        keys_row = jnp.concatenate(
            [jnp.sum(key.astype(F32), axis=0, keepdims=True), pad], axis=1
        )
        out_ref[head] = join(sums - keys * mean, keys, keys_row, mean, lane, extra).astype(BF16)


def join(centred, keys, keys_row, mean, lane, extra):
    size = HEAD_DIM
    high, low = high_low(keys)
    top = jnp.where(
        lane < size, centred, jnp.where(lane == size, high, jnp.where(lane == size + 1, low, 0.0))
    )
    mean_high, mean_low = high_low(mean)
    row_high, row_low = high_low(keys_row)
    bottom = jnp.where(
        extra == 0,
        mean_high,
        jnp.where(extra == 1, mean_low, jnp.where(extra == 2, row_high, jnp.where(extra == 3, row_low, 0.0))),
    )
    return jnp.concatenate([top, bottom], axis=0)


def parts_of(packed):
    size = HEAD_DIM
    top = packed[:size]
    keys = top[:, size : size + 1] + top[:, size + 1 : size + 2]
    mean = packed[size : size + 1] + packed[size + 1 : size + 2]
    keys_row = packed[size + 2 : size + 3] + packed[size + 3 : size + 4]
    return top, keys, keys_row, mean


def merge_packed(first, second, lane, extra):
    top_a, keys_a, row_a, mean_a = parts_of(first)
    top_b, keys_b, row_b, mean_b = parts_of(second)
    mass_a = jnp.sum(keys_a, axis=0, keepdims=True)
    mass_b = jnp.sum(keys_b, axis=0, keepdims=True)
    mean = (mass_a * mean_a + mass_b * mean_b) * guarded(mass_a + mass_b)
    centred = top_a + top_b + keys_a * (mean_a - mean) + keys_b * (mean_b - mean)
    return join(centred, keys_a + keys_b, row_a + row_b, mean, lane, extra)


def merge_body(state_ref, other_ref, out_ref, send_ref):
    size = HEAD_DIM
    lane = lax.broadcasted_iota(jnp.int32, (size, LANES), 1)
    extra = lax.broadcasted_iota(jnp.int32, (LANES - size, LANES), 0)
    for head in range(state_ref.shape[0]):
        merged = merge_packed(
            state_ref[head].astype(F32), other_ref[head].astype(F32), lane, extra
        )
        out_ref[head] = merged
        send_ref[head] = merged.astype(BF16)


def add_body(state_ref, other_ref, out_ref, send_ref):
    size = HEAD_DIM
    lane = lax.broadcasted_iota(jnp.int32, (size, LANES), 1)
    for head in range(state_ref.shape[0]):
        merged = state_ref[head].astype(F32) + other_ref[head].astype(F32)
        sums = merged[:, size : size + 1] + merged[:, size + 1 : size + 2]
        high, low = high_low(sums)
        merged = jnp.where(
            lane < size, merged, jnp.where(lane == size, high, jnp.where(lane == size + 1, low, 0.0))
        )
        out_ref[head] = merged
        send_ref[head] = merged.astype(BF16)


def forward_body(query_ref, grad_ref, local_ref, state_ref, attended_ref, query_grad_ref, out_ref):
    size = HEAD_DIM
    count = query_ref.shape[0]
    lane = lax.broadcasted_iota(jnp.int32, (size, LANES), 1)
    tail = lax.broadcasted_iota(jnp.int32, (count, LANES - size), 1)
    for head in range(HEADS):
        lanes = slice(head * size, (head + 1) * size)
        query_pre = query_ref[:, lanes]
        query = jnp.maximum(query_pre, 0)
        grad = grad_ref[:, lanes]
        cotangent = grad.astype(F32)
        state = state_ref[head]
        mixed = dot(query, state[:size], ((1,), (0,)))
        back = dot(grad, state[:, :size], ((1,), (1,)))
        centred = mixed[:, :size]
        mass = mixed[:, size : size + 1] + mixed[:, size + 1 : size + 2]
        inverse = 1.0 / (mass + 1.0)
        rows = state[size:].astype(F32)
        mean = rows[0:1, :size] + rows[1:2, :size]
        keys_row = rows[2:3, :size] + rows[3:4, :size]
        output = (centred + mass * mean) * inverse
        attended_ref[:, lanes] = (output + local_ref[:, lanes]).astype(BF16)
        along = back[:, size : size + 1] + back[:, size + 1 : size + 2]
        product = jnp.sum(cotangent * centred, axis=1, keepdims=True)
        grad_query = (back[:, :size] + ((along - product) * inverse) * keys_row) * inverse
        query_grad_ref[:, lanes] = jnp.where(
            query_pre.astype(F32) > 0, grad_query, 0.0
        ).astype(BF16)
        high, low = high_low(-(product + mass * along) * inverse)
        side = jnp.where(tail == 0, high, jnp.where(tail == 1, low, 0.0)).astype(BF16)
        scaled = (query.astype(F32) * inverse).astype(BF16)
        sums = dot(scaled, jnp.concatenate([grad, side], axis=1), ((0,), (0,)))
        total = sums[:, size : size + 1] + sums[:, size + 1 : size + 2]
        high, low = high_low(total)
        out_ref[head] = jnp.where(
            lane < size, sums, jnp.where(lane == size, high, jnp.where(lane == size + 1, low, 0.0))
        ).astype(BF16)


def backward_body(key_ref, value_ref, conv_ref, state_ref, key_grad_ref, value_grad_ref):
    size = HEAD_DIM
    count = key_ref.shape[0]
    ones = jnp.where(
        lax.broadcasted_iota(jnp.int32, (count, LANES - size), 1) < 2, 1.0, 0.0
    ).astype(BF16)
    for head in range(HEADS):
        lanes = slice(head * size, (head + 1) * size)
        key_pre = key_ref[:, lanes]
        state = state_ref[head]
        value = jnp.concatenate([value_ref[:, lanes], ones], axis=1)
        grad_key = dot(value, state, ((1,), (1,)))
        mixed = dot(jnp.maximum(key_pre, 0), state, ((1,), (0,)))
        key_grad_ref[:, lanes] = jnp.where(key_pre.astype(F32) > 0, grad_key, 0.0).astype(BF16)
        value_grad_ref[:, lanes] = (mixed[:, :size] + conv_ref[:, lanes]).astype(BF16)


def with_edges(block):
    count = lax.axis_size("space")
    forward = [(i, i + 1) for i in range(count - 1)]
    backward = [(i + 1, i) for i in range(count - 1)]
    low = lax.ppermute(block[:, -1:], "space", forward)
    high = lax.ppermute(block[:, :1], "space", backward)
    return jnp.concatenate([low, block, high], axis=1)


def scan_over(local, body, reverse):
    half = local.shape[0] // 2
    place = lax.axis_index("space")
    count = lax.axis_size("tm")
    swap = [(0, 1), (1, 0)]
    own = lax.dynamic_slice_in_dim(local, place * half, half, 0)
    away = lax.dynamic_slice_in_dim(local, (1 - place) * half, half, 0)
    shape = (struct(own.shape, F32), struct(own.shape, BF16))
    state, send = call(body, shape, own, lax.ppermute(away, "space", swap))
    step = 1
    while step < count:
        pairs = [(i, i + step) for i in range(count - step)]
        if reverse:
            pairs = [(b, a) for a, b in pairs]
        state, send = call(body, shape, state, lax.ppermute(send, "tm", pairs))
        step *= 2
    other = lax.ppermute(send, "space", swap)
    return jnp.where(
        place == 0, jnp.concatenate([send, other], 0), jnp.concatenate([other, send], 0)
    )


def shards(query_pre, key_pre, value_pre, grad_out, conv_taps):
    frames, rows, cols, width = value_pre.shape
    assert frames == 1 and width == HEADS * HEAD_DIM and lax.axis_size("space") == 2
    count = rows * cols
    flat = (count, width)
    query, key, value, grad = (
        a.reshape(flat) for a in (query_pre, key_pre, value_pre, grad_out)
    )
    partial = call(partial_body, struct((HEADS, LANES, LANES), BF16), key, value)
    value_rows = with_edges(value_pre).reshape((rows + 2) * cols, width)
    grad_rows = with_edges(grad_out).reshape((rows + 2) * cols, width)
    local, conv, taps_grad = call(
        lambda *refs: conv_body(rows, cols, *refs),
        (struct(flat, F32), struct(flat, F32), struct((9, width), F32)),
        value_rows,
        grad_rows,
        conv_taps.reshape(9, width),
    )
    taps_grad = lax.psum(taps_grad, ("tm", "space")).reshape(3, 3, width)
    state = scan_over(partial, merge_body, False)
    attended, query_grad, grad_partial = call(
        forward_body,
        (struct(flat, BF16), struct(flat, BF16), struct((HEADS, HEAD_DIM, LANES), BF16)),
        query,
        grad,
        local,
        state,
    )
    grad_state = scan_over(grad_partial, add_body, True)
    key_grad, value_grad = call(
        backward_body,
        (struct(flat, BF16), struct(flat, BF16)),
        key,
        value,
        conv,
        grad_state,
    )
    full = value_pre.shape
    return (
        attended.reshape(full),
        query_grad.reshape(full),
        key_grad.reshape(full),
        value_grad.reshape(full),
        taps_grad,
    )


def solution(mesh):
    tokens = P(("groups", "tm"), "space", None, None)
    return jax.shard_map(
        shards,
        mesh=mesh,
        in_specs=(tokens, tokens, tokens, tokens, P()),
        out_specs=(tokens, tokens, tokens, tokens, P("groups", None, None)),
        check_vma=False,
    )
```

time: 256 us -> 250 us (0.977)
  blocking collectives: 77.6 us -> 0 us
  Pallas kernels: 0 us -> 58.1 us
  waiting for transfers between devices: 78.7 us -> 132 us
  other arithmetic: 26.9 us -> 4.97 us
  local copies, waits for them, and re-layouts: 26.9 us -> 12.5 us
  starting transfers between devices: 13.8 us -> 26.2 us
  matrix products: 12.1 us -> 0 us
    all_gather x6 -> x0, blocking collectives: 72.1 us -> none  [the longest x1 31.9 us: carried_in(): gathered = jax.tree.map(lambda a: lax.all_gather(a, axis), part)]
    psum x1, waiting for transfers between devices: 14.3 us -> 74.7 us  [shards(): taps_grad = lax.psum(taps_grad, ('tm', 'space')).reshape(3, 3, width)]
    pallas_call x0 -> x12, Pallas kernels: none -> 58.1 us  [call(): pl.pallas_call(body, out_shape=out_shape, in_specs=[pl.BlockSpec(memory_s...]
    ppermute x4 -> x14, waiting for transfers between devices: 0.01 us -> 57.1 us  [the longest x6 53.6 us: scan_over(): state, send = call(body, shape, state, lax.ppermute(send, 'tm', pairs))]
    all_gather x2 -> x0, waiting for transfers between devices: 37.5 us -> none  [the longest x1 37.5 us: carried_in(): gathered = jax.tree.map(lambda a: lax.all_gather(a, axis), part)]
    reduce_scatter x2 -> x0, waiting for transfers between devices: 26.8 us -> none  [the longest x1 15.5 us: shards(): lax.psum_scatter(grad_partial, 'space', scatter_dimension=0, tiled=True)]
    ppermute x4 -> x14, starting transfers between devices: 9.31 us -> 26.1 us  [the longest x6 19.5 us: scan_over(): state, send = call(body, shape, state, lax.ppermute(send, 'tm', pairs))]
    reshape x12 -> x2, local copies, waits for them, and re-layouts: 14.7 us -> 1.39 us  [the longest x1 0.7 us: shards(): conv_taps.reshape(9, width)]
  transfers between devices with their start and end apart: 11 -> 15, of which waited for: 4 -> 10; matrix products, arithmetic and copies ran while one was open for 23% -> 2% of each run, Pallas kernels for 0% -> 10%
where the time goes in v1:
time: 250 us; the launch traced here: 248 us
  waiting for transfers between devices  132 us (53%)
  Pallas kernels  58.1 us (23%)
  starting transfers between devices  26.2 us (10%)
  between operations  14.2 us (6%)
  local copies, waits for them, and re-layouts  12.5 us (5%)
  other arithmetic  4.97 us (2%)
    psum x1, waiting for transfers between devices, shards(): taps_grad = lax.psum(taps_grad, ('tm', 'space')).reshape(3, 3, width)  74.7 us
    pallas_call x12, Pallas kernels, call(): pl.pallas_call(body, out_shape=out_shape, in_specs=[pl.BlockSpec(memory_s...  58.1 us
    ppermute x6, waiting for transfers between devices, scan_over(): state, send = call(body, shape, state, lax.ppermute(send, 'tm', pairs))  53.6 us
    ppermute x6, starting transfers between devices, scan_over(): state, send = call(body, shape, state, lax.ppermute(send, 'tm', pairs))  19.5 us
    unnamed x27, local copies, waits for them, and re-layouts  7.31 us
  transfers between devices with their start and end apart: 15, of which 10 were waited for; matrix products, arithmetic and copies ran while one was open for 2% of the time, Pallas kernels for 10%

profile of v1, /device:TPU:0, one launch (start us, length us, event | category | flops | bytes accessed | tf_op | source)
XLA Modules:
  0.0 247.7 jit_solution(18211091483341841250)
XLA Ops:
  7.2 4.5 %shard_map.93 = bf16[20,128,128]{2,1,0:T(8,128)(2,1)} custom-call(bf16[128,2240]{1,0:T(8,128)(2,1)} %bitcast.15, bf16[128,2240]{1,0:T(8,128)(2,1)} %bitcast.10), custom_call_target="tpu_custom_call" | custom-call | tf_op jit(solution)/shard_map/pallas_call | solution.py:17
  11.8 1.9 constant_dynamic-slice_fusion.2
  16.1 3.6 %shard_map.94 = (f32[10,128,128]{2,1,0:T(8,128)}, bf16[10,128,128]{2,1,0:T(8,128)(2,1)}) custom-call(bf16[10,128,128]{2,1,0:T(8,128)(2,1)} %get-tuple-element.50.state_ref, bf16[10,128,128]{2,1,0:T(8,128)(2,1)} %copy-done.2), custom_call_target="tpu_custom_call" | custom-call | tf_op jit(solution)/shard_map/pallas_call | solution.py:17
  19.7 4.9 %collective-permute-start.5 = (bf16[10,128,128]{2,1,0:T(8,128)(2,1)}, bf16[10,128,128]{2,1,0:T(8,128)(2,1)S(1)}, u32[]{:S(2)}, u32[]{:S(2)}) collective-permute-start(bf16[10,128,128]{2,1,0:T(8,128)(2,1)} %get-tuple-element.29), channel_id=1, source_target_pairs={{0,2},{2,4},{4,6},{6,8},{8,10},{10,12},{12,14},{1,3},{3,5},{5,7},{... | collective-permute-start | bytes 983048 | tf_op jit(solution)/shard_map/ppermute | solution.py:241
  24.7 1.8 collective-permute-start.2
  26.5 1.3 collective-permute-start.3
  27.8 4.4 %collective-permute-done.5.other_ref = bf16[10,128,128]{2,1,0:T(8,128)(2,1)S(1)} collective-permute-done((bf16[10,128,128]{2,1,0:T(8,128)(2,1)}, bf16[10,128,128]{2,1,0:T(8,128)(2,1)S(1)}, u32[]{:S(2)}, u32[]{:S(2)}) %collective-permute-start.5) | collective-permute-done | bytes 327712 | tf_op jit(solution)/shard_map/ppermute | solution.py:241
  32.9 3.8 %shard_map.95 = (f32[10,128,128]{2,1,0:T(8,128)}, bf16[10,128,128]{2,1,0:T(8,128)(2,1)}) custom-call(f32[10,128,128]{2,1,0:T(8,128)} %get-tuple-element.28.state_ref, bf16[10,128,128]{2,1,0:T(8,128)(2,1)} %copy-done.5), custom_call_target="tpu_custom_call" | custom-call | tf_op jit(solution)/shard_map/pallas_call | solution.py:17
  36.7 5.2 %collective-permute-start.6 = (bf16[10,128,128]{2,1,0:T(8,128)(2,1)}, bf16[10,128,128]{2,1,0:T(8,128)(2,1)S(1)}, u32[]{:S(2)}, u32[]{:S(2)}) collective-permute-start(bf16[10,128,128]{2,1,0:T(8,128)(2,1)} %get-tuple-element.31), channel_id=1, source_target_pairs={{0,4},{2,6},{4,8},{6,10},{8,12},{10,14},{1,5},{3,7},{5,9},{7,11},{... | collective-permute-start | bytes 983048 | tf_op jit(solution)/shard_map/ppermute | solution.py:241
  42.0 1.3 collective-permute-start
  43.3 1.3 collective-permute-start.1
  45.3 3.3 %collective-permute-done.6.other_ref = bf16[10,128,128]{2,1,0:T(8,128)(2,1)S(1)} collective-permute-done((bf16[10,128,128]{2,1,0:T(8,128)(2,1)}, bf16[10,128,128]{2,1,0:T(8,128)(2,1)S(1)}, u32[]{:S(2)}, u32[]{:S(2)}) %collective-permute-start.6) | collective-permute-done | bytes 327712 | tf_op jit(solution)/shard_map/ppermute | solution.py:241
  49.4 3.8 %shard_map.96 = (f32[10,128,128]{2,1,0:T(8,128)}, bf16[10,128,128]{2,1,0:T(8,128)(2,1)}) custom-call(f32[10,128,128]{2,1,0:T(8,128)} %get-tuple-element.30.state_ref, bf16[10,128,128]{2,1,0:T(8,128)(2,1)} %copy-done.4), custom_call_target="tpu_custom_call" | custom-call | tf_op jit(solution)/shard_map/pallas_call | solution.py:17
  53.2 5.5 %collective-permute-start.7 = (bf16[10,128,128]{2,1,0:T(8,128)(2,1)}, bf16[10,128,128]{2,1,0:T(8,128)(2,1)S(1)}, u32[]{:S(2)}, u32[]{:S(2)}) collective-permute-start(bf16[10,128,128]{2,1,0:T(8,128)(2,1)} %get-tuple-element.33), channel_id=1, source_target_pairs={{0,8},{2,10},{4,12},{6,14},{1,9},{3,11},{5,13},{7,15},{16,24},{18,... | collective-permute-start | bytes 983048 | tf_op jit(solution)/shard_map/ppermute | solution.py:241
  59.7 4.6 %collective-permute-done.7.other_ref = bf16[10,128,128]{2,1,0:T(8,128)(2,1)S(1)} collective-permute-done((bf16[10,128,128]{2,1,0:T(8,128)(2,1)}, bf16[10,128,128]{2,1,0:T(8,128)(2,1)S(1)}, u32[]{:S(2)}, u32[]{:S(2)}) %collective-permute-start.7) | collective-permute-done | bytes 327712 | tf_op jit(solution)/shard_map/ppermute | solution.py:241
  65.1 3.8 %shard_map.97 = (f32[10,128,128]{2,1,0:T(8,128)}, bf16[10,128,128]{2,1,0:T(8,128)(2,1)}) custom-call(f32[10,128,128]{2,1,0:T(8,128)} %get-tuple-element.32.state_ref, bf16[10,128,128]{2,1,0:T(8,128)(2,1)} %copy-done.6), custom_call_target="tpu_custom_call" | custom-call | tf_op jit(solution)/shard_map/pallas_call | solution.py:17
  69.9 5.3 %shard_map.92 = (f32[128,2240]{1,0:T(8,128)}, f32[128,2240]{1,0:T(8,128)}, f32[9,2240]{1,0:T(8,128)}) custom-call(bf16[192,2240]{1,0:T(8,128)(2,1)} %bitcast.14, bf16[192,2240]{1,0:T(8,128)(2,1)} %bitcast.13, f32[9,2240]{1,0:T(8,128)} %reshape.50.refs_2_), custom_call_target="tpu_custom_call" | custom-call | tf_op jit(solution)/shard_map/pallas_call | solution.py:17
  76.2 14.1 %shard_map.98 = (bf16[128,2240]{1,0:T(8,128)(2,1)}, bf16[128,2240]{1,0:T(8,128)(2,1)}, bf16[20,112,128]{2,1,0:T(8,128)(2,1)}) custom-call(bf16[128,2240]{1,0:T(8,128)(2,1)} %bitcast.17, bf16[128,2240]{1,0:T(8,128)(2,1)} %bitcast.12, f32[128,2240]{1,0:T(8,128)} %get-tuple-element.27.local_ref, bf16[20,128,128]{2,1,0:T(8,128)(2,1)} %maximum_select_fusion.state_ref), custom_call_target="tpu_custom_call" | custom-call | tf_op jit(solution)/shard_map/pallas_call | solution.py:17
  90.3 1.8 constant_dynamic-slice_fusion
  94.5 2.9 %shard_map.99 = (f32[10,112,128]{2,1,0:T(8,128)}, bf16[10,112,128]{2,1,0:T(8,128)(2,1)}) custom-call(bf16[10,112,128]{2,1,0:T(8,128)(2,1)} %get-tuple-element.56.state_ref, bf16[10,112,128]{2,1,0:T(8,128)(2,1)} %copy-done.7), custom_call_target="tpu_custom_call" | custom-call | tf_op jit(solution)/shard_map/pallas_call | solution.py:17
  97.4 1.3 collective-permute-start.10
  98.7 9.9 %collective-permute-done.10.other_ref = bf16[10,112,128]{2,1,0:T(8,128)(2,1)S(1)} collective-permute-done((bf16[10,112,128]{2,1,0:T(8,128)(2,1)}, bf16[10,112,128]{2,1,0:T(8,128)(2,1)S(1)}, u32[]{:S(2)}, u32[]{:S(2)}) %collective-permute-start.10) | collective-permute-done | bytes 286752 | tf_op jit(solution)/shard_map/ppermute | solution.py:241
  109.3 3.0 %shard_map.100 = (f32[10,112,128]{2,1,0:T(8,128)}, bf16[10,112,128]{2,1,0:T(8,128)(2,1)}) custom-call(f32[10,112,128]{2,1,0:T(8,128)} %get-tuple-element.39.state_ref, bf16[10,112,128]{2,1,0:T(8,128)(2,1)} %copy-done.8), custom_call_target="tpu_custom_call" | custom-call | tf_op jit(solution)/shard_map/pallas_call | solution.py:17
  112.3 1.3 collective-permute-start.11
  113.6 15.8 %collective-permute-done.11.other_ref = bf16[10,112,128]{2,1,0:T(8,128)(2,1)S(1)} collective-permute-done((bf16[10,112,128]{2,1,0:T(8,128)(2,1)}, bf16[10,112,128]{2,1,0:T(8,128)(2,1)S(1)}, u32[]{:S(2)}, u32[]{:S(2)}) %collective-permute-start.11) | collective-permute-done | bytes 286752 | tf_op jit(solution)/shard_map/ppermute | solution.py:241
  130.1 3.0 %shard_map.101 = (f32[10,112,128]{2,1,0:T(8,128)}, bf16[10,112,128]{2,1,0:T(8,128)(2,1)}) custom-call(f32[10,112,128]{2,1,0:T(8,128)} %get-tuple-element.41.state_ref, bf16[10,112,128]{2,1,0:T(8,128)(2,1)} %copy-done.9), custom_call_target="tpu_custom_call" | custom-call | tf_op jit(solution)/shard_map/pallas_call | solution.py:17
  134.4 15.5 %collective-permute-done.12.other_ref = bf16[10,112,128]{2,1,0:T(8,128)(2,1)S(1)} collective-permute-done((bf16[10,112,128]{2,1,0:T(8,128)(2,1)}, bf16[10,112,128]{2,1,0:T(8,128)(2,1)S(1)}, u32[]{:S(2)}, u32[]{:S(2)}) %collective-permute-start.12) | collective-permute-done | bytes 286752 | tf_op jit(solution)/shard_map/ppermute | solution.py:241
  150.6 3.0 %shard_map.102 = (f32[10,112,128]{2,1,0:T(8,128)}, bf16[10,112,128]{2,1,0:T(8,128)(2,1)}) custom-call(f32[10,112,128]{2,1,0:T(8,128)} %get-tuple-element.43.state_ref, bf16[10,112,128]{2,1,0:T(8,128)(2,1)} %copy-done.10), custom_call_target="tpu_custom_call" | custom-call | tf_op jit(solution)/shard_map/pallas_call | solution.py:17
  155.4 2.0 maximum_select_fusion.1.state_ref
  157.4 7.3 %shard_map.103 = (bf16[128,2240]{1,0:T(8,128)(2,1)}, bf16[128,2240]{1,0:T(8,128)(2,1)}) custom-call(bf16[128,2240]{1,0:T(8,128)(2,1)} %bitcast.16, bf16[128,2240]{1,0:T(8,128)(2,1)} %bitcast.11, f32[128,2240]{1,0:T(8,128)} %get-tuple-element.37.conv_ref, bf16[20,112,128]{2,1,0:T(8,128)(2,1)} %maximum_select_fusion.1.state_ref), custom_call_target="tpu_custom_call" | custom-call | tf_op jit(solution)/shard_map/pallas_call | solution.py:17
  164.6 74.7 %all-reduce.2.cloned.1.call-done = f32[3,3,2240]{2,1,0:T(4,128)} async-done(((f32[3,3,2240]{2,1,0:T(4,128)}), f32[3,3,2240]{2,1,0:T(4,128)}) %all-reduce.2.cloned.1.call-update) | async-done | bytes 80656 | tf_op jit(solution)/shard_map/psum | solution.py:267
  239.3 1.6 copy.11
  (48 shorter events, 16.1 us)
Async XLA Ops:
  7.2 232.1 %all-reduce.2.cloned.1.call-start = ((), (), s32[]{:S(2)}) async-start(), calls=%async_computation | async-start | bytes 221184 | tf_op jit(solution)/shard_map/psum | solution.py:267
  11.7 12.9 %copy-start.1 = (bf16[1,4,32,2240]{3,2,1,0:T(8,128)(2,1)S(1)}, bf16[1,4,32,2240]{3,2,1,0:T(8,128)(2,1)}, u32[]{:S(2)}) copy-start(bf16[1,4,32,2240]{3,2,1,0:T(8,128)(2,1)} %param.8) | copy-start | bytes 1720324
  13.7 28.3 %copy-start = (bf16[1,4,32,2240]{3,2,1,0:T(8,128)(2,1)S(1)}, bf16[1,4,32,2240]{3,2,1,0:T(8,128)(2,1)}, u32[]{:S(2)}) copy-start(bf16[1,4,32,2240]{3,2,1,0:T(8,128)(2,1)} %param.7) | copy-start | bytes 1720324
  13.7 1.7 collective-permute-start.4
  15.4 0.7 copy-start.2
  19.7 24.9 %copy-start.12 = (f32[3,3,2240]{2,1,0:T(4,128)S(1)}, f32[3,3,2240]{2,1,0:T(4,128)}, u32[]{:S(2)}) copy-start(f32[3,3,2240]{2,1,0:T(4,128)} %param.9) | copy-start | bytes 241924
  19.7 12.5 %collective-permute-start.5 = (bf16[10,128,128]{2,1,0:T(8,128)(2,1)}, bf16[10,128,128]{2,1,0:T(8,128)(2,1)S(1)}, u32[]{:S(2)}, u32[]{:S(2)}) collective-permute-start(bf16[10,128,128]{2,1,0:T(8,128)(2,1)} %get-tuple-element.29), channel_id=1, source_target_pairs={{0,2},{2,4},{4,6},{6,8},{8,10},{10,12},{12,14},{1,3},{3,5},{5,7},{... | collective-permute-start | bytes 983048 | tf_op jit(solution)/shard_map/ppermute | solution.py:241
  24.7 34.0 %collective-permute-start.2 = (bf16[1,1,32,2240]{3,2,1,0:T(8,128)(2,1)S(1)}, bf16[1,1,32,2240]{3,2,1,0:T(8,128)(2,1)S(1)}, u32[]{:S(2)}, u32[]{:S(2)}) collective-permute-start(bf16[1,1,32,2240]{3,2,1,0:T(8,128)(2,1)S(1)} %get-tuple-element.51), channel_id=1, source_target_pairs={{0,1},{2,3},{4,5},{6,7},{8,9},{10,11},{12,13},{14,15},{16,17},{18,... | collective-permute-start | bytes 430088 | tf_op jit(solution)/shard_map/ppermute | solution.py:222
  26.5 32.2 %collective-permute-start.3 = (bf16[1,1,32,2240]{3,2,1,0:T(8,128)(2,1)S(1)}, bf16[1,1,32,2240]{3,2,1,0:T(8,128)(2,1)S(1)}, u32[]{:S(2)}, u32[]{:S(2)}) collective-permute-start(bf16[1,1,32,2240]{3,2,1,0:T(8,128)(2,1)S(1)} %get-tuple-element.52), channel_id=1, source_target_pairs={{1,0},{3,2},{5,4},{7,6},{9,8},{11,10},{13,12},{15,14},{17,16},{19,... | collective-permute-start | bytes 430088 | tf_op jit(solution)/shard_map/ppermute | solution.py:223
  32.2 0.7 copy-start.5
  36.7 11.9 %collective-permute-start.6 = (bf16[10,128,128]{2,1,0:T(8,128)(2,1)}, bf16[10,128,128]{2,1,0:T(8,128)(2,1)S(1)}, u32[]{:S(2)}, u32[]{:S(2)}) collective-permute-start(bf16[10,128,128]{2,1,0:T(8,128)(2,1)} %get-tuple-element.31), channel_id=1, source_target_pairs={{0,4},{2,6},{4,8},{6,10},{8,12},{10,14},{1,5},{3,7},{5,9},{7,11},{... | collective-permute-start | bytes 983048 | tf_op jit(solution)/shard_map/ppermute | solution.py:241
  42.0 26.9 %collective-permute-start = (bf16[1,1,32,2240]{3,2,1,0:T(8,128)(2,1)S(1)}, bf16[1,1,32,2240]{3,2,1,0:T(8,128)(2,1)S(1)}, u32[]{:S(2)}, u32[]{:S(2)}) collective-permute-start(bf16[1,1,32,2240]{3,2,1,0:T(8,128)(2,1)S(1)} %get-tuple-element.53), channel_id=1, source_target_pairs={{0,1},{2,3},{4,5},{6,7},{8,9},{10,11},{12,13},{14,15},{16,17},{18,... | collective-permute-start | bytes 430088 | tf_op jit(solution)/shard_map/ppermute | solution.py:222
  43.3 25.6 %collective-permute-start.1 = (bf16[1,1,32,2240]{3,2,1,0:T(8,128)(2,1)S(1)}, bf16[1,1,32,2240]{3,2,1,0:T(8,128)(2,1)S(1)}, u32[]{:S(2)}, u32[]{:S(2)}) collective-permute-start(bf16[1,1,32,2240]{3,2,1,0:T(8,128)(2,1)S(1)} %get-tuple-element.54), channel_id=1, source_target_pairs={{1,0},{3,2},{5,4},{7,6},{9,8},{11,10},{13,12},{15,14},{17,16},{19,... | collective-permute-start | bytes 430088 | tf_op jit(solution)/shard_map/ppermute | solution.py:223
  48.7 0.7 copy-start.4
  53.2 11.2 %collective-permute-start.7 = (bf16[10,128,128]{2,1,0:T(8,128)(2,1)}, bf16[10,128,128]{2,1,0:T(8,128)(2,1)S(1)}, u32[]{:S(2)}, u32[]{:S(2)}) collective-permute-start(bf16[10,128,128]{2,1,0:T(8,128)(2,1)} %get-tuple-element.33), channel_id=1, source_target_pairs={{0,8},{2,10},{4,12},{6,14},{1,9},{3,11},{5,13},{7,15},{16,24},{18,... | collective-permute-start | bytes 983048 | tf_op jit(solution)/shard_map/ppermute | solution.py:241
  64.4 0.7 copy-start.6
  68.9 6.4 %collective-permute-start.8 = (bf16[10,128,128]{2,1,0:T(8,128)(2,1)}, bf16[10,128,128]{2,1,0:T(8,128)(2,1)S(1)}, u32[]{:S(2)}, u32[]{:S(2)}) collective-permute-start(bf16[10,128,128]{2,1,0:T(8,128)(2,1)} %get-tuple-element.34), channel_id=1, source_target_pairs={{0,1},{1,0},{2,3},{3,2},{4,5},{5,4},{6,7},{7,6},{8,9},{9,8},{10,11... | collective-permute-start | bytes 983048 | tf_op jit(solution)/shard_map/ppermute | solution.py:243
  69.9 5.3 %copy-start.3 = (bf16[10,128,128]{2,1,0:T(8,128)(2,1)S(1)}, bf16[10,128,128]{2,1,0:T(8,128)(2,1)}, u32[]{:S(2)}) copy-start(bf16[10,128,128]{2,1,0:T(8,128)(2,1)} %get-tuple-element.34) | copy-start | bytes 983044
  92.1 1.7 collective-permute-start.9
  93.8 0.7 copy-start.7
  97.4 11.2 %collective-permute-start.10 = (bf16[10,112,128]{2,1,0:T(8,128)(2,1)}, bf16[10,112,128]{2,1,0:T(8,128)(2,1)S(1)}, u32[]{:S(2)}, u32[]{:S(2)}) collective-permute-start(bf16[10,112,128]{2,1,0:T(8,128)(2,1)} %get-tuple-element.40), channel_id=1, source_target_pairs={{2,0},{4,2},{6,4},{8,6},{10,8},{12,10},{14,12},{3,1},{5,3},{7,5},{... | collective-permute-start | bytes 860168 | tf_op jit(solution)/shard_map/ppermute | solution.py:241
  108.6 0.7 copy-start.8
  109.3 44.3 %copy-start.11 = (f32[9,2240]{1,0:T(8,128)S(1)}, f32[9,2240]{1,0:T(8,128)}, u32[]{:S(2)}) copy-start(f32[9,2240]{1,0:T(8,128)} %get-tuple-element.48) | copy-start | bytes 241924
  112.3 17.1 %collective-permute-start.11 = (bf16[10,112,128]{2,1,0:T(8,128)(2,1)}, bf16[10,112,128]{2,1,0:T(8,128)(2,1)S(1)}, u32[]{:S(2)}, u32[]{:S(2)}) collective-permute-start(bf16[10,112,128]{2,1,0:T(8,128)(2,1)} %get-tuple-element.42), channel_id=1, source_target_pairs={{4,0},{6,2},{8,4},{10,6},{12,8},{14,10},{5,1},{7,3},{9,5},{11,7},{... | collective-permute-start | bytes 860168 | tf_op jit(solution)/shard_map/ppermute | solution.py:241
  129.4 0.7 copy-start.9
  133.1 16.8 %collective-permute-start.12 = (bf16[10,112,128]{2,1,0:T(8,128)(2,1)}, bf16[10,112,128]{2,1,0:T(8,128)(2,1)S(1)}, u32[]{:S(2)}, u32[]{:S(2)}) collective-permute-start(bf16[10,112,128]{2,1,0:T(8,128)(2,1)} %get-tuple-element.44), channel_id=1, source_target_pairs={{8,0},{10,2},{12,4},{14,6},{9,1},{11,3},{13,5},{15,7},{24,16},{26,... | collective-permute-start | bytes 860168 | tf_op jit(solution)/shard_map/ppermute | solution.py:241
  149.9 0.7 copy-start.10
  153.6 1.8 collective-permute-start.13
Sparse Core Ops, SparseCore 0:
  154.5 84.8 all-reduce.1

commit v2 on v1

--- a/solution.py
+++ b/solution.py
@@ -246,6 +246,17 @@
     )
 
 
+def summed_over(x, axis):
+    count = lax.axis_size(axis)
+    if count & (count - 1):
+        return lax.psum(x, axis)
+    step = 1
+    while step < count:
+        x = x + lax.ppermute(x, axis, [(i, i ^ step) for i in range(count)])
+        step *= 2
+    return x
+
+
 def shards(query_pre, key_pre, value_pre, grad_out, conv_taps):
     frames, rows, cols, width = value_pre.shape
     assert frames == 1 and width == HEADS * HEAD_DIM and lax.axis_size("space") == 2
@@ -264,7 +275,9 @@
         grad_rows,
         conv_taps.reshape(9, width),
     )
-    taps_grad = lax.psum(taps_grad, ("tm", "space")).reshape(3, 3, width)
+    for axis in ("space", "tm"):
+        taps_grad = summed_over(taps_grad, axis)
+    taps_grad = taps_grad.reshape(3, 3, width)
     state = scan_over(partial, merge_body, False)
     attended, query_grad, grad_partial = call(
         forward_body,

time: 250 us -> 177 us (0.71)
  waiting for transfers between devices: 132 us -> 74.5 us
  between operations: 14.2 us -> 0.87 us
    psum x1 -> x0, waiting for transfers between devices: 74.7 us -> none  [shards(): taps_grad = lax.psum(taps_grad, ('tm', 'space')).reshape(3, 3, width)]
    ppermute x0 -> x4, waiting for transfers between devices: none -> 18.5 us  [summed_over(): x = x + lax.ppermute(x, axis, [(i, i ^ step) for i in range(count)])]
    unnamed x27 -> x28, local copies, waits for them, and re-layouts: 7.31 us -> 5.79 us
  transfers between devices with their start and end apart: 15 -> 18, of which waited for: 10 -> 11; matrix products, arithmetic and copies ran while one was open for 2% -> 2% of each run, Pallas kernels for 10% -> 11%
where the time goes in v2:
time: 177 us
  waiting for transfers between devices  74.5 us (42%)
  Pallas kernels  58 us (33%)
  starting transfers between devices  28.2 us (16%)
  local copies, waits for them, and re-layouts  10.9 us (6%)
  other arithmetic  4 us (2%)
    pallas_call x12, Pallas kernels, call(): pl.pallas_call(body, out_shape=out_shape, in_specs=[pl.BlockSpec(memory_s...  58 us
    ppermute x6, waiting for transfers between devices, scan_over(): state, send = call(body, shape, state, lax.ppermute(send, 'tm', pairs))  53.5 us
    ppermute x6, starting transfers between devices, scan_over(): state, send = call(body, shape, state, lax.ppermute(send, 'tm', pairs))  19.5 us
    ppermute x4, waiting for transfers between devices, summed_over(): x = x + lax.ppermute(x, axis, [(i, i ^ step) for i in range(count)])  18.5 us
    unnamed x28, local copies, waits for them, and re-layouts  5.79 us
    dynamic_slice x2, local copies, waits for them, and re-layouts, scan_over(): away = lax.dynamic_slice_in_dim(local, (1 - place) * half, half, 0)  3.71 us
  transfers between devices with their start and end apart: 18, of which 11 were waited for; matrix products, arithmetic and copies ran while one was open for 2% of the time, Pallas kernels for 11%

profile of v2, /device:TPU:0, one launch (start us, length us, event | category | flops | bytes accessed | tf_op | source)
XLA Modules:
  0.0 176.5 jit_solution(7013721583264439762)
XLA Ops:
  0.6 4.5 %shard_map.93 = bf16[20,128,128]{2,1,0:T(8,128)(2,1)} custom-call(bf16[128,2240]{1,0:T(8,128)(2,1)} %bitcast.15, bf16[128,2240]{1,0:T(8,128)(2,1)} %bitcast.10), custom_call_target="tpu_custom_call" | custom-call | tf_op jit(solution)/shard_map/pallas_call | solution.py:17
  5.2 1.9 %constant_dynamic-slice_fusion.2 = (bf16[10,128,128]{2,1,0:T(8,128)(2,1)S(1)}, bf16[10,128,128]{2,1,0:T(8,128)(2,1)}) fusion(bf16[20,128,128]{2,1,0:T(8,128)(2,1)} %shard_map.93, s32[]{:T(128)S(6)} %select_n.26, s32[]{:T(128)S(6)} %select_n.25), kind=kLoop, calls=%fused_computation.6 | loop fusion | bytes 1310728 | tf_op jit(solution)/shard_map/dynamic_slice | solution.py:233
  9.6 3.6 %shard_map.94 = (f32[10,128,128]{2,1,0:T(8,128)}, bf16[10,128,128]{2,1,0:T(8,128)(2,1)}) custom-call(bf16[10,128,128]{2,1,0:T(8,128)(2,1)} %get-tuple-element.50.state_ref, bf16[10,128,128]{2,1,0:T(8,128)(2,1)} %copy-done.2), custom_call_target="tpu_custom_call" | custom-call | tf_op jit(solution)/shard_map/pallas_call | solution.py:17
  13.2 4.9 %collective-permute-start.5 = (bf16[10,128,128]{2,1,0:T(8,128)(2,1)}, bf16[10,128,128]{2,1,0:T(8,128)(2,1)S(1)}, u32[]{:S(2)}, u32[]{:S(2)}) collective-permute-start(bf16[10,128,128]{2,1,0:T(8,128)(2,1)} %get-tuple-element.29), channel_id=1, source_target_pairs={{0,2},{2,4},{4,6},{6,8},{8,10},{10,12},{12,14},{1,3},{3,5},{5,7},{... | collective-permute-start | bytes 983048 | tf_op jit(solution)/shard_map/ppermute | solution.py:241
  18.1 1.8 %collective-permute-start.2 = (bf16[1,1,32,2240]{3,2,1,0:T(8,128)(2,1)S(1)}, bf16[1,1,32,2240]{3,2,1,0:T(8,128)(2,1)S(1)}, u32[]{:S(2)}, u32[]{:S(2)}) collective-permute-start(bf16[1,1,32,2240]{3,2,1,0:T(8,128)(2,1)S(1)} %get-tuple-element.51), channel_id=1, source_target_pairs={{0,1},{2,3},{4,5},{6,7},{8,9},{10,11},{12,13},{14,15},{16,17},{18,... | collective-permute-start | bytes 430088 | tf_op jit(solution)/shard_map/ppermute | solution.py:222
  19.9 1.3 collective-permute-start.3
  21.2 4.4 %collective-permute-done.5.other_ref = bf16[10,128,128]{2,1,0:T(8,128)(2,1)S(1)} collective-permute-done((bf16[10,128,128]{2,1,0:T(8,128)(2,1)}, bf16[10,128,128]{2,1,0:T(8,128)(2,1)S(1)}, u32[]{:S(2)}, u32[]{:S(2)}) %collective-permute-start.5) | collective-permute-done | bytes 327712 | tf_op jit(solution)/shard_map/ppermute | solution.py:241
  26.4 3.8 %shard_map.95 = (f32[10,128,128]{2,1,0:T(8,128)}, bf16[10,128,128]{2,1,0:T(8,128)(2,1)}) custom-call(f32[10,128,128]{2,1,0:T(8,128)} %get-tuple-element.28.state_ref, bf16[10,128,128]{2,1,0:T(8,128)(2,1)} %copy-done.5), custom_call_target="tpu_custom_call" | custom-call | tf_op jit(solution)/shard_map/pallas_call | solution.py:17
  30.1 5.2 %collective-permute-start.6 = (bf16[10,128,128]{2,1,0:T(8,128)(2,1)}, bf16[10,128,128]{2,1,0:T(8,128)(2,1)S(1)}, u32[]{:S(2)}, u32[]{:S(2)}) collective-permute-start(bf16[10,128,128]{2,1,0:T(8,128)(2,1)} %get-tuple-element.31), channel_id=1, source_target_pairs={{0,4},{2,6},{4,8},{6,10},{8,12},{10,14},{1,5},{3,7},{5,9},{7,11},{... | collective-permute-start | bytes 983048 | tf_op jit(solution)/shard_map/ppermute | solution.py:241
  35.4 1.3 collective-permute-start
  36.7 1.3 collective-permute-start.1
  38.8 3.3 %collective-permute-done.6.other_ref = bf16[10,128,128]{2,1,0:T(8,128)(2,1)S(1)} collective-permute-done((bf16[10,128,128]{2,1,0:T(8,128)(2,1)}, bf16[10,128,128]{2,1,0:T(8,128)(2,1)S(1)}, u32[]{:S(2)}, u32[]{:S(2)}) %collective-permute-start.6) | collective-permute-done | bytes 327712 | tf_op jit(solution)/shard_map/ppermute | solution.py:241
  42.8 3.8 %shard_map.96 = (f32[10,128,128]{2,1,0:T(8,128)}, bf16[10,128,128]{2,1,0:T(8,128)(2,1)}) custom-call(f32[10,128,128]{2,1,0:T(8,128)} %get-tuple-element.30.state_ref, bf16[10,128,128]{2,1,0:T(8,128)(2,1)} %copy-done.4), custom_call_target="tpu_custom_call" | custom-call | tf_op jit(solution)/shard_map/pallas_call | solution.py:17
  46.6 5.5 %collective-permute-start.7 = (bf16[10,128,128]{2,1,0:T(8,128)(2,1)}, bf16[10,128,128]{2,1,0:T(8,128)(2,1)S(1)}, u32[]{:S(2)}, u32[]{:S(2)}) collective-permute-start(bf16[10,128,128]{2,1,0:T(8,128)(2,1)} %get-tuple-element.33), channel_id=1, source_target_pairs={{0,8},{2,10},{4,12},{6,14},{1,9},{3,11},{5,13},{7,15},{16,24},{18,... | collective-permute-start | bytes 983048 | tf_op jit(solution)/shard_map/ppermute | solution.py:241
  53.1 4.6 %collective-permute-done.7.other_ref = bf16[10,128,128]{2,1,0:T(8,128)(2,1)S(1)} collective-permute-done((bf16[10,128,128]{2,1,0:T(8,128)(2,1)}, bf16[10,128,128]{2,1,0:T(8,128)(2,1)S(1)}, u32[]{:S(2)}, u32[]{:S(2)}) %collective-permute-start.7) | collective-permute-done | bytes 327712 | tf_op jit(solution)/shard_map/ppermute | solution.py:241
  58.5 3.8 %shard_map.97 = (f32[10,128,128]{2,1,0:T(8,128)}, bf16[10,128,128]{2,1,0:T(8,128)(2,1)}) custom-call(f32[10,128,128]{2,1,0:T(8,128)} %get-tuple-element.32.state_ref, bf16[10,128,128]{2,1,0:T(8,128)(2,1)} %copy-done.6), custom_call_target="tpu_custom_call" | custom-call | tf_op jit(solution)/shard_map/pallas_call | solution.py:17
  63.3 5.3 %shard_map.92 = (f32[128,2240]{1,0:T(8,128)}, f32[128,2240]{1,0:T(8,128)}, f32[9,2240]{1,0:T(8,128)}) custom-call(bf16[192,2240]{1,0:T(8,128)(2,1)} %bitcast.14, bf16[192,2240]{1,0:T(8,128)(2,1)} %bitcast.13, f32[9,2240]{1,0:T(8,128)} %reshape.50.refs_2_), custom_call_target="tpu_custom_call" | custom-call | tf_op jit(solution)/shard_map/pallas_call | solution.py:17
  69.6 14.1 %shard_map.98 = (bf16[128,2240]{1,0:T(8,128)(2,1)}, bf16[128,2240]{1,0:T(8,128)(2,1)}, bf16[20,112,128]{2,1,0:T(8,128)(2,1)}) custom-call(bf16[128,2240]{1,0:T(8,128)(2,1)} %bitcast.17, bf16[128,2240]{1,0:T(8,128)(2,1)} %bitcast.12, f32[128,2240]{1,0:T(8,128)} %get-tuple-element.27.local_ref, bf16[20,128,128]{2,1,0:T(8,128)(2,1)} %maximum_select_fusion.state_ref), custom_call_target="tpu_custom_call" | custom-call | tf_op jit(solution)/shard_map/pallas_call | solution.py:17
  83.8 1.8 %constant_dynamic-slice_fusion = (bf16[10,112,128]{2,1,0:T(8,128)(2,1)S(1)}, bf16[10,112,128]{2,1,0:T(8,128)(2,1)}) fusion(bf16[20,112,128]{2,1,0:T(8,128)(2,1)} %get-tuple-element.38, s32[]{:T(128)S(6)} %select_n.26, s32[]{:T(128)S(6)} %select_n.25), kind=kLoop, calls=%fused_computation.4 | loop fusion | bytes 1146888 | tf_op jit(solution)/shard_map/dynamic_slice | solution.py:233
  88.0 2.9 %shard_map.99 = (f32[10,112,128]{2,1,0:T(8,128)}, bf16[10,112,128]{2,1,0:T(8,128)(2,1)}) custom-call(bf16[10,112,128]{2,1,0:T(8,128)(2,1)} %get-tuple-element.56.state_ref, bf16[10,112,128]{2,1,0:T(8,128)(2,1)} %copy-done.7), custom_call_target="tpu_custom_call" | custom-call | tf_op jit(solution)/shard_map/pallas_call | solution.py:17
  90.9 1.3 collective-permute-start.10
  92.2 9.9 %collective-permute-done.10.other_ref = bf16[10,112,128]{2,1,0:T(8,128)(2,1)S(1)} collective-permute-done((bf16[10,112,128]{2,1,0:T(8,128)(2,1)}, bf16[10,112,128]{2,1,0:T(8,128)(2,1)S(1)}, u32[]{:S(2)}, u32[]{:S(2)}) %collective-permute-start.10) | collective-permute-done | bytes 286752 | tf_op jit(solution)/shard_map/ppermute | solution.py:241
  102.8 3.0 %shard_map.100 = (f32[10,112,128]{2,1,0:T(8,128)}, bf16[10,112,128]{2,1,0:T(8,128)(2,1)}) custom-call(f32[10,112,128]{2,1,0:T(8,128)} %get-tuple-element.39.state_ref, bf16[10,112,128]{2,1,0:T(8,128)(2,1)} %copy-done.9), custom_call_target="tpu_custom_call" | custom-call | tf_op jit(solution)/shard_map/pallas_call | solution.py:17
  107.1 15.8 %collective-permute-done.11.other_ref = bf16[10,112,128]{2,1,0:T(8,128)(2,1)S(1)} collective-permute-done((bf16[10,112,128]{2,1,0:T(8,128)(2,1)}, bf16[10,112,128]{2,1,0:T(8,128)(2,1)S(1)}, u32[]{:S(2)}, u32[]{:S(2)}) %collective-permute-start.11) | collective-permute-done | bytes 286752 | tf_op jit(solution)/shard_map/ppermute | solution.py:241
  123.6 3.0 %shard_map.101 = (f32[10,112,128]{2,1,0:T(8,128)}, bf16[10,112,128]{2,1,0:T(8,128)(2,1)}) custom-call(f32[10,112,128]{2,1,0:T(8,128)} %get-tuple-element.41.state_ref, bf16[10,112,128]{2,1,0:T(8,128)(2,1)} %copy-done.10), custom_call_target="tpu_custom_call" | custom-call | tf_op jit(solution)/shard_map/pallas_call | solution.py:17
  127.9 15.4 %collective-permute-done.12.other_ref = bf16[10,112,128]{2,1,0:T(8,128)(2,1)S(1)} collective-permute-done((bf16[10,112,128]{2,1,0:T(8,128)(2,1)}, bf16[10,112,128]{2,1,0:T(8,128)(2,1)S(1)}, u32[]{:S(2)}, u32[]{:S(2)}) %collective-permute-start.12) | collective-permute-done | bytes 286752 | tf_op jit(solution)/shard_map/ppermute | solution.py:241
  144.1 3.0 %shard_map.102 = (f32[10,112,128]{2,1,0:T(8,128)}, bf16[10,112,128]{2,1,0:T(8,128)(2,1)}) custom-call(f32[10,112,128]{2,1,0:T(8,128)} %get-tuple-element.43.state_ref, bf16[10,112,128]{2,1,0:T(8,128)(2,1)} %copy-done.8), custom_call_target="tpu_custom_call" | custom-call | tf_op jit(solution)/shard_map/pallas_call | solution.py:17
  147.1 1.8 %collective-permute-start.15 = (f32[9,2240]{1,0:T(8,128)S(1)}, f32[9,2240]{1,0:T(8,128)S(1)}, u32[]{:S(2)}, u32[]{:S(2)}) collective-permute-start(f32[9,2240]{1,0:T(8,128)S(1)} %add.22), channel_id=1, source_target_pairs={{0,2},{2,0},{4,6},{6,4},{8,10},{10,8},{12,14},{14,12},{1,3},{3,1},... | collective-permute-start | bytes 241928 | tf_op jit(solution)/shard_map/ppermute | solution.py:255
  148.9 4.5 %collective-permute-done.15 = f32[9,2240]{1,0:T(8,128)S(1)} collective-permute-done((f32[9,2240]{1,0:T(8,128)S(1)}, f32[9,2240]{1,0:T(8,128)S(1)}, u32[]{:S(2)}, u32[]{:S(2)}) %collective-permute-start.15) | collective-permute-done | bytes 80672 | tf_op jit(solution)/shard_map/ppermute | solution.py:255
  153.6 5.4 %collective-permute-done.16 = f32[9,2240]{1,0:T(8,128)S(1)} collective-permute-done((f32[9,2240]{1,0:T(8,128)S(1)}, f32[9,2240]{1,0:T(8,128)S(1)}, u32[]{:S(2)}, u32[]{:S(2)}) %collective-permute-start.16) | collective-permute-done | bytes 80672 | tf_op jit(solution)/shard_map/ppermute | solution.py:255
  159.1 8.6 %collective-permute-done.17 = f32[9,2240]{1,0:T(8,128)S(1)} collective-permute-done((f32[9,2240]{1,0:T(8,128)S(1)}, f32[9,2240]{1,0:T(8,128)S(1)}, u32[]{:S(2)}, u32[]{:S(2)}) %collective-permute-start.17) | collective-permute-done | bytes 80672 | tf_op jit(solution)/shard_map/ppermute | solution.py:255
  169.3 7.2 %shard_map.103 = (bf16[128,2240]{1,0:T(8,128)(2,1)}, bf16[128,2240]{1,0:T(8,128)(2,1)}) custom-call(bf16[128,2240]{1,0:T(8,128)(2,1)} %bitcast.16, bf16[128,2240]{1,0:T(8,128)(2,1)} %bitcast.11, f32[128,2240]{1,0:T(8,128)} %get-tuple-element.37.conv_ref, bf16[20,112,128]{2,1,0:T(8,128)(2,1)} %maximum_select_fusion.1.state_ref), custom_call_target="tpu_custom_call" | custom-call | tf_op jit(solution)/shard_map/pallas_call | solution.py:17
  (58 shorter events, 17.5 us)
Async XLA Ops:
  5.2 12.9 %copy-start.1 = (bf16[1,4,32,2240]{3,2,1,0:T(8,128)(2,1)S(1)}, bf16[1,4,32,2240]{3,2,1,0:T(8,128)(2,1)}, u32[]{:S(2)}) copy-start(bf16[1,4,32,2240]{3,2,1,0:T(8,128)(2,1)} %param.8) | copy-start | bytes 1720324
  7.1 28.3 %copy-start = (bf16[1,4,32,2240]{3,2,1,0:T(8,128)(2,1)S(1)}, bf16[1,4,32,2240]{3,2,1,0:T(8,128)(2,1)}, u32[]{:S(2)}) copy-start(bf16[1,4,32,2240]{3,2,1,0:T(8,128)(2,1)} %param.7) | copy-start | bytes 1720324
  7.1 1.8 collective-permute-start.4
  8.8 0.7 copy-start.2
  13.2 24.9 %copy-start.13 = (f32[3,3,2240]{2,1,0:T(4,128)S(1)}, f32[3,3,2240]{2,1,0:T(4,128)}, u32[]{:S(2)}) copy-start(f32[3,3,2240]{2,1,0:T(4,128)} %param.9) | copy-start | bytes 241924
  13.2 12.5 %collective-permute-start.5 = (bf16[10,128,128]{2,1,0:T(8,128)(2,1)}, bf16[10,128,128]{2,1,0:T(8,128)(2,1)S(1)}, u32[]{:S(2)}, u32[]{:S(2)}) collective-permute-start(bf16[10,128,128]{2,1,0:T(8,128)(2,1)} %get-tuple-element.29), channel_id=1, source_target_pairs={{0,2},{2,4},{4,6},{6,8},{8,10},{10,12},{12,14},{1,3},{3,5},{5,7},{... | collective-permute-start | bytes 983048 | tf_op jit(solution)/shard_map/ppermute | solution.py:241
  18.1 34.0 %collective-permute-start.2 = (bf16[1,1,32,2240]{3,2,1,0:T(8,128)(2,1)S(1)}, bf16[1,1,32,2240]{3,2,1,0:T(8,128)(2,1)S(1)}, u32[]{:S(2)}, u32[]{:S(2)}) collective-permute-start(bf16[1,1,32,2240]{3,2,1,0:T(8,128)(2,1)S(1)} %get-tuple-element.51), channel_id=1, source_target_pairs={{0,1},{2,3},{4,5},{6,7},{8,9},{10,11},{12,13},{14,15},{16,17},{18,... | collective-permute-start | bytes 430088 | tf_op jit(solution)/shard_map/ppermute | solution.py:222
  19.9 32.2 %collective-permute-start.3 = (bf16[1,1,32,2240]{3,2,1,0:T(8,128)(2,1)S(1)}, bf16[1,1,32,2240]{3,2,1,0:T(8,128)(2,1)S(1)}, u32[]{:S(2)}, u32[]{:S(2)}) collective-permute-start(bf16[1,1,32,2240]{3,2,1,0:T(8,128)(2,1)S(1)} %get-tuple-element.52), channel_id=1, source_target_pairs={{1,0},{3,2},{5,4},{7,6},{9,8},{11,10},{13,12},{15,14},{17,16},{19,... | collective-permute-start | bytes 430088 | tf_op jit(solution)/shard_map/ppermute | solution.py:223
  25.6 0.7 copy-start.5
  30.1 11.9 %collective-permute-start.6 = (bf16[10,128,128]{2,1,0:T(8,128)(2,1)}, bf16[10,128,128]{2,1,0:T(8,128)(2,1)S(1)}, u32[]{:S(2)}, u32[]{:S(2)}) collective-permute-start(bf16[10,128,128]{2,1,0:T(8,128)(2,1)} %get-tuple-element.31), channel_id=1, source_target_pairs={{0,4},{2,6},{4,8},{6,10},{8,12},{10,14},{1,5},{3,7},{5,9},{7,11},{... | collective-permute-start | bytes 983048 | tf_op jit(solution)/shard_map/ppermute | solution.py:241
  35.4 26.9 %collective-permute-start = (bf16[1,1,32,2240]{3,2,1,0:T(8,128)(2,1)S(1)}, bf16[1,1,32,2240]{3,2,1,0:T(8,128)(2,1)S(1)}, u32[]{:S(2)}, u32[]{:S(2)}) collective-permute-start(bf16[1,1,32,2240]{3,2,1,0:T(8,128)(2,1)S(1)} %get-tuple-element.53), channel_id=1, source_target_pairs={{0,1},{2,3},{4,5},{6,7},{8,9},{10,11},{12,13},{14,15},{16,17},{18,... | collective-permute-start | bytes 430088 | tf_op jit(solution)/shard_map/ppermute | solution.py:222
  36.7 25.6 %collective-permute-start.1 = (bf16[1,1,32,2240]{3,2,1,0:T(8,128)(2,1)S(1)}, bf16[1,1,32,2240]{3,2,1,0:T(8,128)(2,1)S(1)}, u32[]{:S(2)}, u32[]{:S(2)}) collective-permute-start(bf16[1,1,32,2240]{3,2,1,0:T(8,128)(2,1)S(1)} %get-tuple-element.54), channel_id=1, source_target_pairs={{1,0},{3,2},{5,4},{7,6},{9,8},{11,10},{13,12},{15,14},{17,16},{19,... | collective-permute-start | bytes 430088 | tf_op jit(solution)/shard_map/ppermute | solution.py:223
  42.1 0.7 copy-start.4
  46.6 11.2 %collective-permute-start.7 = (bf16[10,128,128]{2,1,0:T(8,128)(2,1)}, bf16[10,128,128]{2,1,0:T(8,128)(2,1)S(1)}, u32[]{:S(2)}, u32[]{:S(2)}) collective-permute-start(bf16[10,128,128]{2,1,0:T(8,128)(2,1)} %get-tuple-element.33), channel_id=1, source_target_pairs={{0,8},{2,10},{4,12},{6,14},{1,9},{3,11},{5,13},{7,15},{16,24},{18,... | collective-permute-start | bytes 983048 | tf_op jit(solution)/shard_map/ppermute | solution.py:241
  57.8 0.7 copy-start.6
  62.3 6.4 %collective-permute-start.8 = (bf16[10,128,128]{2,1,0:T(8,128)(2,1)}, bf16[10,128,128]{2,1,0:T(8,128)(2,1)S(1)}, u32[]{:S(2)}, u32[]{:S(2)}) collective-permute-start(bf16[10,128,128]{2,1,0:T(8,128)(2,1)} %get-tuple-element.34), channel_id=1, source_target_pairs={{0,1},{1,0},{2,3},{3,2},{4,5},{5,4},{6,7},{7,6},{8,9},{9,8},{10,11... | collective-permute-start | bytes 983048 | tf_op jit(solution)/shard_map/ppermute | solution.py:243
  63.3 5.3 %copy-start.3 = (bf16[10,128,128]{2,1,0:T(8,128)(2,1)S(1)}, bf16[10,128,128]{2,1,0:T(8,128)(2,1)}, u32[]{:S(2)}) copy-start(bf16[10,128,128]{2,1,0:T(8,128)(2,1)} %get-tuple-element.34) | copy-start | bytes 983044
  85.5 42.3 %copy-start.12 = (f32[9,2240]{1,0:T(8,128)S(1)}, f32[9,2240]{1,0:T(8,128)}, u32[]{:S(2)}) copy-start(f32[9,2240]{1,0:T(8,128)} %get-tuple-element.48) | copy-start | bytes 241924
  85.5 1.7 collective-permute-start.9
  87.3 0.7 copy-start.7
  90.9 11.2 %collective-permute-start.10 = (bf16[10,112,128]{2,1,0:T(8,128)(2,1)}, bf16[10,112,128]{2,1,0:T(8,128)(2,1)S(1)}, u32[]{:S(2)}, u32[]{:S(2)}) collective-permute-start(bf16[10,112,128]{2,1,0:T(8,128)(2,1)} %get-tuple-element.40), channel_id=1, source_target_pairs={{2,0},{4,2},{6,4},{8,6},{10,8},{12,10},{14,12},{3,1},{5,3},{7,5},{... | collective-permute-start | bytes 860168 | tf_op jit(solution)/shard_map/ppermute | solution.py:241
  102.1 0.7 copy-start.9
  105.8 17.1 %collective-permute-start.11 = (bf16[10,112,128]{2,1,0:T(8,128)(2,1)}, bf16[10,112,128]{2,1,0:T(8,128)(2,1)S(1)}, u32[]{:S(2)}, u32[]{:S(2)}) collective-permute-start(bf16[10,112,128]{2,1,0:T(8,128)(2,1)} %get-tuple-element.42), channel_id=1, source_target_pairs={{4,0},{6,2},{8,4},{10,6},{12,8},{14,10},{5,1},{7,3},{9,5},{11,7},{... | collective-permute-start | bytes 860168 | tf_op jit(solution)/shard_map/ppermute | solution.py:241
  122.8 0.7 copy-start.10
  126.6 16.8 %collective-permute-start.12 = (bf16[10,112,128]{2,1,0:T(8,128)(2,1)}, bf16[10,112,128]{2,1,0:T(8,128)(2,1)S(1)}, u32[]{:S(2)}, u32[]{:S(2)}) collective-permute-start(bf16[10,112,128]{2,1,0:T(8,128)(2,1)} %get-tuple-element.44), channel_id=1, source_target_pairs={{8,0},{10,2},{12,4},{14,6},{9,1},{11,3},{13,5},{15,7},{24,16},{26,... | collective-permute-start | bytes 860168 | tf_op jit(solution)/shard_map/ppermute | solution.py:241
  127.9 19.2 %collective-permute-start.14 = (f32[9,2240]{1,0:T(8,128)S(1)}, f32[9,2240]{1,0:T(8,128)S(1)}, u32[]{:S(2)}, u32[]{:S(2)}) collective-permute-start(f32[9,2240]{1,0:T(8,128)S(1)} %copy-done.12), channel_id=1, source_target_pairs={{0,1},{1,0},{2,3},{3,2},{4,5},{5,4},{6,7},{7,6},{8,9},{9,8},{10,11... | collective-permute-start | bytes 241928 | tf_op jit(solution)/shard_map/ppermute | solution.py:255
  143.4 0.7 copy-start.8
  147.1 21.3 %copy-start.11 = (bf16[10,112,128]{2,1,0:T(8,128)(2,1)S(1)}, bf16[10,112,128]{2,1,0:T(8,128)(2,1)}, u32[]{:S(2)}) copy-start(bf16[10,112,128]{2,1,0:T(8,128)(2,1)} %get-tuple-element.45) | copy-start | bytes 860164
  147.1 21.3 %collective-permute-start.13 = (bf16[10,112,128]{2,1,0:T(8,128)(2,1)}, bf16[10,112,128]{2,1,0:T(8,128)(2,1)S(1)}, u32[]{:S(2)}, u32[]{:S(2)}) collective-permute-start(bf16[10,112,128]{2,1,0:T(8,128)(2,1)} %get-tuple-element.45), channel_id=1, source_target_pairs={{0,1},{1,0},{2,3},{3,2},{4,5},{5,4},{6,7},{7,6},{8,9},{9,8},{10,11... | collective-permute-start | bytes 860168 | tf_op jit(solution)/shard_map/ppermute | solution.py:243
  147.1 6.3 %collective-permute-start.15 = (f32[9,2240]{1,0:T(8,128)S(1)}, f32[9,2240]{1,0:T(8,128)S(1)}, u32[]{:S(2)}, u32[]{:S(2)}) collective-permute-start(f32[9,2240]{1,0:T(8,128)S(1)} %add.22), channel_id=1, source_target_pairs={{0,2},{2,0},{4,6},{6,4},{8,10},{10,8},{12,14},{14,12},{1,3},{3,1},... | collective-permute-start | bytes 241928 | tf_op jit(solution)/shard_map/ppermute | solution.py:255
  153.5 5.5 %collective-permute-start.16 = (f32[9,2240]{1,0:T(8,128)S(1)}, f32[9,2240]{1,0:T(8,128)S(1)}, u32[]{:S(2)}, u32[]{:S(2)}) collective-permute-start(f32[9,2240]{1,0:T(8,128)S(1)} %add.23), channel_id=1, source_target_pairs={{0,4},{2,6},{4,0},{6,2},{8,12},{10,14},{12,8},{14,10},{1,5},{3,7},... | collective-permute-start | bytes 241928 | tf_op jit(solution)/shard_map/ppermute | solution.py:255
  159.0 8.7 %collective-permute-start.17 = (f32[9,2240]{1,0:T(8,128)S(1)}, f32[9,2240]{1,0:T(8,128)S(1)}, u32[]{:S(2)}, u32[]{:S(2)}) collective-permute-start(f32[9,2240]{1,0:T(8,128)S(1)} %add.24), channel_id=1, source_target_pairs={{0,8},{2,10},{4,12},{6,14},{8,0},{10,2},{12,4},{14,6},{1,9},{3,11}... | collective-permute-start | bytes 241928 | tf_op jit(solution)/shard_map/ppermute | solution.py:255

commit v3 on v2

--- a/solution.py
+++ b/solution.py
@@ -1,3 +1,5 @@
+import functools
+
 import jax
 import jax.numpy as jnp
 from jax import lax
@@ -11,6 +13,12 @@
 F32 = jnp.float32
 BF16 = jnp.bfloat16
 VMEM_LIMIT = 60 * 1024 * 1024
+
+
+def cost(microseconds):
+    return pl.CostEstimate(
+        flops=int(microseconds * 1e9), bytes_accessed=int(microseconds * 3e6), transcendentals=0
+    )
 
 
 def call(body, out_shape, *args):
@@ -20,6 +28,7 @@
         in_specs=[pl.BlockSpec(memory_space=pltpu.VMEM)] * len(args),
         out_specs=jax.tree.map(lambda _: pl.BlockSpec(memory_space=pltpu.VMEM), out_shape),
         compiler_params=pltpu.CompilerParams(vmem_limit_bytes=VMEM_LIMIT),
+        cost_estimate=cost(6),
     )(*args)
 
 
@@ -133,30 +142,150 @@
     return join(centred, keys_a + keys_b, row_a + row_b, mean, lane, extra)
 
 
-def merge_body(state_ref, other_ref, out_ref, send_ref):
-    size = HEAD_DIM
-    lane = lax.broadcasted_iota(jnp.int32, (size, LANES), 1)
-    extra = lax.broadcasted_iota(jnp.int32, (LANES - size, LANES), 0)
-    for head in range(state_ref.shape[0]):
-        merged = merge_packed(
-            state_ref[head].astype(F32), other_ref[head].astype(F32), lane, extra
+def add_packed(first, second, lane, extra):
+    size = HEAD_DIM
+    merged = first + second
+    sums = merged[:, size : size + 1] + merged[:, size + 1 : size + 2]
+    high, low = high_low(sums)
+    return jnp.where(
+        lane < size, merged, jnp.where(lane == size, high, jnp.where(lane == size + 1, low, 0.0))
+    )
+
+
+def scan_body(
+    merge,
+    reverse,
+    local_ref,
+    out_ref,
+    half_ref,
+    core_recv,
+    pair_send,
+    pair_recv,
+    chain_send,
+    chain_recv,
+    core_sems,
+    pair_sems,
+    chain_sems,
+    out_sems,
+):
+    heads = core_recv.shape[0]
+    core = lax.axis_index("space")
+    place = lax.axis_index("tm")
+    links = lax.axis_size("tm") // 2
+    link, side = place // 2, place % 2
+    pair = link * 2 + (1 - side)
+    if reverse:
+        order, ahead, behind, sums_both = links - 1 - link, place - 2, place + 2, side == 0
+    else:
+        order, ahead, behind, sums_both = link, place + 2, place - 2, side == 1
+    lane = lax.broadcasted_iota(jnp.int32, (HEAD_DIM, LANES), 1)
+    extra = lax.broadcasted_iota(jnp.int32, (LANES - HEAD_DIM, LANES), 0)
+
+    def remote(source, target, sems, head, device):
+        return pltpu.make_async_remote_copy(
+            src_ref=source,
+            dst_ref=target,
+            send_sem=sems.at[0, head],
+            recv_sem=sems.at[1, head],
+            device_id=device,
+            device_id_type=pl.DeviceIdType.MESH,
         )
-        out_ref[head] = merged
-        send_ref[head] = merged.astype(BF16)
-
-
-def add_body(state_ref, other_ref, out_ref, send_ref):
-    size = HEAD_DIM
-    lane = lax.broadcasted_iota(jnp.int32, (size, LANES), 1)
-    for head in range(state_ref.shape[0]):
-        merged = state_ref[head].astype(F32) + other_ref[head].astype(F32)
-        sums = merged[:, size : size + 1] + merged[:, size + 1 : size + 2]
-        high, low = high_low(sums)
-        merged = jnp.where(
-            lane < size, merged, jnp.where(lane == size, high, jnp.where(lane == size + 1, low, 0.0))
+
+    def core_copy(head):
+        return remote(
+            local_ref.at[(1 - core) * heads + head],
+            core_recv.at[head],
+            core_sems,
+            head,
+            {"space": 1 - core},
         )
-        out_ref[head] = merged
-        send_ref[head] = merged.astype(BF16)
+
+    def pair_copy(head):
+        return remote(pair_send.at[head], pair_recv.at[head], pair_sems, head, {"tm": pair})
+
+    def chain_copy(head):
+        return remote(chain_send.at[head], chain_recv.at[head], chain_sems, head, {"tm": ahead})
+
+    def out_copy(head):
+        mine = out_ref.at[core * heads + head]
+        return remote(mine, mine, out_sems, head, {"space": 1 - core})
+
+    barrier = pltpu.get_barrier_semaphore()
+
+    def greet(device):
+        pl.semaphore_signal(barrier, inc=1, device_id=device, device_id_type=pl.DeviceIdType.MESH)
+
+    greet({"space": 1 - core})
+    greet({"tm": pair})
+
+    @pl.when(order < links - 1)
+    def _():
+        greet({"tm": ahead})
+
+    @pl.when(order > 0)
+    def _():
+        greet({"tm": behind})
+
+    @pl.when(order == 0)
+    def _():
+        chain_recv[...] = jnp.zeros_like(chain_recv)
+
+    peers = 2 + jnp.minimum(order, 1) + jnp.minimum(links - 1 - order, 1)
+    pl.semaphore_wait(barrier, peers)
+
+    def begin(head, _):
+        core_copy(head).start()
+        return 0
+
+    lax.fori_loop(0, heads, begin, 0)
+
+    def over_cores(head, _):
+        core_copy(head).wait_recv()
+        half = merge(
+            local_ref[core * heads + head].astype(F32), core_recv[head].astype(F32), lane, extra
+        )
+        half_ref[head] = half
+        pair_send[head] = half.astype(BF16)
+        pair_copy(head).start()
+        return 0
+
+    lax.fori_loop(0, heads, over_cores, 0)
+
+    def over_pairs(head, _):
+        pair_copy(head).wait_recv()
+        half = half_ref[head]
+        both = merge(half, pair_recv[head].astype(F32), lane, extra)
+
+        @pl.when(order > 0)
+        def _():
+            chain_copy(head).wait_recv()
+
+        before = chain_recv[head].astype(F32)
+
+        @pl.when(order < links - 1)
+        def _():
+            chain_send[head] = merge(before, both, lane, extra).astype(BF16)
+            chain_copy(head).start()
+
+        mine = jnp.where(sums_both, both, half)
+        out_ref[core * heads + head] = merge(before, mine, lane, extra).astype(BF16)
+        out_copy(head).start()
+        return 0
+
+    lax.fori_loop(0, heads, over_pairs, 0)
+
+    def finish(head, _):
+        core_copy(head).wait_send()
+        pair_copy(head).wait_send()
+
+        @pl.when(order < links - 1)
+        def _():
+            chain_copy(head).wait_send()
+
+        out_copy(head).wait()
+        return 0
+
+    lax.fori_loop(0, heads, finish, 0)
 
 
 def forward_body(query_ref, grad_ref, local_ref, state_ref, attended_ref, query_grad_ref, out_ref):
@@ -224,26 +353,20 @@
     return jnp.concatenate([low, block, high], axis=1)
 
 
-def scan_over(local, body, reverse):
-    half = local.shape[0] // 2
-    place = lax.axis_index("space")
-    count = lax.axis_size("tm")
-    swap = [(0, 1), (1, 0)]
-    own = lax.dynamic_slice_in_dim(local, place * half, half, 0)
-    away = lax.dynamic_slice_in_dim(local, (1 - place) * half, half, 0)
-    shape = (struct(own.shape, F32), struct(own.shape, BF16))
-    state, send = call(body, shape, own, lax.ppermute(away, "space", swap))
-    step = 1
-    while step < count:
-        pairs = [(i, i + step) for i in range(count - step)]
-        if reverse:
-            pairs = [(b, a) for a, b in pairs]
-        state, send = call(body, shape, state, lax.ppermute(send, "tm", pairs))
-        step *= 2
-    other = lax.ppermute(send, "space", swap)
-    return jnp.where(
-        place == 0, jnp.concatenate([send, other], 0), jnp.concatenate([other, send], 0)
-    )
+def scan_over(local, merge, reverse):
+    half = (local.shape[0] // 2,) + local.shape[1:]
+    sems = pltpu.SemaphoreType.DMA((2, half[0]))
+    return pl.pallas_call(
+        functools.partial(scan_body, merge, reverse),
+        out_shape=struct(local.shape, BF16),
+        in_specs=[pl.BlockSpec(memory_space=pltpu.VMEM)],
+        out_specs=pl.BlockSpec(memory_space=pltpu.VMEM),
+        scratch_shapes=[pltpu.VMEM(half, F32)] + [pltpu.VMEM(half, BF16)] * 5 + [sems] * 4,
+        compiler_params=pltpu.CompilerParams(
+            collective_id=int(reverse), has_side_effects=True, vmem_limit_bytes=VMEM_LIMIT
+        ),
+        cost_estimate=cost(25),
+    )(local)
 
 
 def summed_over(x, axis):
@@ -260,6 +383,7 @@
 def shards(query_pre, key_pre, value_pre, grad_out, conv_taps):
     frames, rows, cols, width = value_pre.shape
     assert frames == 1 and width == HEADS * HEAD_DIM and lax.axis_size("space") == 2
+    assert lax.axis_size("tm") % 2 == 0
     count = rows * cols
     flat = (count, width)
     query, key, value, grad = (
@@ -278,7 +402,7 @@
     for axis in ("space", "tm"):
         taps_grad = summed_over(taps_grad, axis)
     taps_grad = taps_grad.reshape(3, 3, width)
-    state = scan_over(partial, merge_body, False)
+    state = scan_over(partial, merge_packed, False)
     attended, query_grad, grad_partial = call(
         forward_body,
         (struct(flat, BF16), struct(flat, BF16), struct((HEADS, HEAD_DIM, LANES), BF16)),
@@ -287,7 +411,7 @@
         local,
         state,
     )
-    grad_state = scan_over(grad_partial, add_body, True)
+    grad_state = scan_over(grad_partial, add_packed, True)
     key_grad, value_grad = call(
         backward_body,
         (struct(flat, BF16), struct(flat, BF16)),

time: 177 us -> 99.2 us (0.56)
  waiting for transfers between devices: 74.5 us -> 0.5 us
  Pallas kernels: 58 us -> 77.8 us
  starting transfers between devices: 28.2 us -> 14.1 us
  local copies, waits for them, and re-layouts: 10.9 us -> 3.42 us
  other arithmetic: 4 us -> 2.16 us
    ppermute x10 -> x0, waiting for transfers between devices: 56 us -> none  [the longest x6 53.5 us: scan_over(): state, send = call(body, shape, state, lax.ppermute(send, 'tm', pairs))]
    pallas_call x0 -> x2, Pallas kernels: none -> 46.8 us  [scan_over(): pl.pallas_call(functools.partial(scan_body, merge, reverse), out_shape=st...]
    pallas_call x12 -> x4, Pallas kernels: 58 us -> 31 us  [call(): pl.pallas_call(body, out_shape=out_shape, in_specs=[pl.BlockSpec(memory_s...]
    ppermute x10 -> x0, starting transfers between devices: 20.5 us -> none  [the longest x6 19.5 us: scan_over(): state, send = call(body, shape, state, lax.ppermute(send, 'tm', pairs))]
    ppermute x4, waiting for transfers between devices: 18.5 us -> 0.49 us  [summed_over(): x = x + lax.ppermute(x, axis, [(i, i ^ step) for i in range(count)])]
    unnamed x28 -> x8, local copies, waits for them, and re-layouts: 5.79 us -> 0.02 us
    ppermute x4, starting transfers between devices: 2.04 us -> 6.08 us  [summed_over(): x = x + lax.ppermute(x, axis, [(i, i ^ step) for i in range(count)])]
    dynamic_slice x2 -> x0, local copies, waits for them, and re-layouts: 3.71 us -> none  [scan_over(): away = lax.dynamic_slice_in_dim(local, (1 - place) * half, half, 0)]
  transfers between devices with their start and end apart: 18 -> 8, of which waited for: 11 -> 1; matrix products, arithmetic and copies ran while one was open for 2% -> 3% of each run, Pallas kernels for 11% -> 73%
where the time goes in v3:
time: 99.2 us; the launch traced here: 98.8 us
  Pallas kernels  77.8 us (78%)
  starting transfers between devices  14.1 us (14%)
  local copies, waits for them, and re-layouts  3.42 us (3%)
  other arithmetic  2.16 us (2%)
    pallas_call x2, Pallas kernels, scan_over(): pl.pallas_call(functools.partial(scan_body, merge, reverse), out_shape=st...  46.8 us
    pallas_call x4, Pallas kernels, call(): pl.pallas_call(body, out_shape=out_shape, in_specs=[pl.BlockSpec(memory_s...  31 us
    ppermute x4, starting transfers between devices, summed_over(): x = x + lax.ppermute(x, axis, [(i, i ^ step) for i in range(count)])  6.08 us
    ppermute x2, starting transfers between devices, with_edges(): low = lax.ppermute(block[:, -1:], 'space', forward)  5.45 us
    ppermute x2, starting transfers between devices, with_edges(): high = lax.ppermute(block[:, :1], 'space', backward)  2.58 us
    concatenate x2, other arithmetic, with_edges(): return jnp.concatenate([low, block, high], axis=1)  2.09 us
    slice x2, local copies, waits for them, and re-layouts, with_edges(): low = lax.ppermute(block[:, -1:], 'space', forward)  2.01 us
  transfers between devices with their start and end apart: 8, of which 1 were waited for; matrix products, arithmetic and copies ran while one was open for 3% of the time, Pallas kernels for 73%

profile of v3, /device:TPU:0, one launch (start us, length us, event | category | flops | bytes accessed | tf_op | source)
XLA Modules:
  0.0 98.8 jit_solution(6398296927704204850)
XLA Ops:
  0.6 1.0 %fusion.1 = (bf16[1,1,32,2240]{3,2,1,0:T(8,128)(2,1)S(1)}, bf16[1,1,32,2240]{3,2,1,0:T(8,128)(2,1)S(1)}) fusion(bf16[1,4,32,2240]{3,2,1,0:T(8,128)(2,1)} %param.7), kind=kLoop, calls=%fused_computation.3 | loop fusion | bytes 573440 | tf_op jit(solution)/shard_map/slice | solution.py:351
  1.6 2.4 %collective-permute-start = (bf16[1,1,32,2240]{3,2,1,0:T(8,128)(2,1)S(1)}, bf16[1,1,32,2240]{3,2,1,0:T(8,128)(2,1)S(1)}, u32[]{:S(2)}, u32[]{:S(2)}) collective-permute-start(bf16[1,1,32,2240]{3,2,1,0:T(8,128)(2,1)S(1)} %get-tuple-element.23), channel_id=1, source_target_pairs={{0,1},{2,3},{4,5},{6,7},{8,9},{10,11},{12,13},{14,15},{16,17},{18,... | collective-permute-start | bytes 430088 | tf_op jit(solution)/shard_map/ppermute | solution.py:351
  4.1 1.3 %collective-permute-start.1 = (bf16[1,1,32,2240]{3,2,1,0:T(8,128)(2,1)S(1)}, bf16[1,1,32,2240]{3,2,1,0:T(8,128)(2,1)S(1)}, u32[]{:S(2)}, u32[]{:S(2)}) collective-permute-start(bf16[1,1,32,2240]{3,2,1,0:T(8,128)(2,1)S(1)} %get-tuple-element.24), channel_id=1, source_target_pairs={{1,0},{3,2},{5,4},{7,6},{9,8},{11,10},{13,12},{15,14},{17,16},{19,... | collective-permute-start | bytes 430088 | tf_op jit(solution)/shard_map/ppermute | solution.py:352
  5.4 1.0 %fusion = (bf16[1,1,32,2240]{3,2,1,0:T(8,128)(2,1)S(1)}, bf16[1,1,32,2240]{3,2,1,0:T(8,128)(2,1)S(1)}) fusion(bf16[1,4,32,2240]{3,2,1,0:T(8,128)(2,1)} %param.8), kind=kLoop, calls=%fused_computation.2 | loop fusion | bytes 573440 | tf_op jit(solution)/shard_map/slice | solution.py:351
  6.4 3.0 %collective-permute-start.2 = (bf16[1,1,32,2240]{3,2,1,0:T(8,128)(2,1)S(1)}, bf16[1,1,32,2240]{3,2,1,0:T(8,128)(2,1)S(1)}, u32[]{:S(2)}, u32[]{:S(2)}) collective-permute-start(bf16[1,1,32,2240]{3,2,1,0:T(8,128)(2,1)S(1)} %get-tuple-element.21), channel_id=1, source_target_pairs={{0,1},{2,3},{4,5},{6,7},{8,9},{10,11},{12,13},{14,15},{16,17},{18,... | collective-permute-start | bytes 430088 | tf_op jit(solution)/shard_map/ppermute | solution.py:351
  9.4 1.3 %collective-permute-start.3 = (bf16[1,1,32,2240]{3,2,1,0:T(8,128)(2,1)S(1)}, bf16[1,1,32,2240]{3,2,1,0:T(8,128)(2,1)S(1)}, u32[]{:S(2)}, u32[]{:S(2)}) collective-permute-start(bf16[1,1,32,2240]{3,2,1,0:T(8,128)(2,1)S(1)} %get-tuple-element.22), channel_id=1, source_target_pairs={{1,0},{3,2},{5,4},{7,6},{9,8},{11,10},{13,12},{15,14},{17,16},{19,... | collective-permute-start | bytes 430088 | tf_op jit(solution)/shard_map/ppermute | solution.py:352
  10.7 0.0 copy-start.3
  10.7 0.0 copy-start
  10.7 4.6 %shard_map.93.local_ref = bf16[20,128,128]{2,1,0:T(8,128)(2,1)} custom-call(bf16[128,2240]{1,0:T(8,128)(2,1)} %bitcast.16, bf16[128,2240]{1,0:T(8,128)(2,1)} %bitcast.11), custom_call_target="tpu_custom_call" | custom-call | flops 6000000000 | bytes 18000000 | tf_op jit(solution)/shard_map/pallas_call | solution.py:25
  15.3 0.0 copy-done.3
  15.3 0.7 reshape.50.refs_2_
  16.0 0.0 collective-permute-done.2
  16.0 0.0 collective-permute-done.3
  16.0 0.0 copy-done
  16.1 1.0 %pad_maximum_fusion.1 = bf16[1,6,32,2240]{3,2,1,0:T(8,128)(2,1)} fusion(bf16[1,1,32,2240]{3,2,1,0:T(8,128)(2,1)S(1)} %collective-permute-done.3, bf16[1,4,32,2240]{3,2,1,0:T(8,128)(2,1)S(1)} %copy-done, bf16[1,1,32,2240]{3,2,1,0:T(8,128)(2,1)S(1)} %collective-permute-done.2), kind=kLoop, calls=%fused_computation.1 | loop fusion | flops 860160 | bytes 1720320 | tf_op jit(solution)/shard_map/concatenate | solution.py:353
  17.1 0.0 collective-permute-done
  17.1 0.0 collective-permute-done.1
  17.1 1.0 %pad_maximum_fusion = bf16[1,6,32,2240]{3,2,1,0:T(8,128)(2,1)} fusion(bf16[1,1,32,2240]{3,2,1,0:T(8,128)(2,1)S(1)} %collective-permute-done.1, bf16[1,4,32,2240]{3,2,1,0:T(8,128)(2,1)S(1)} %copy-done.1, bf16[1,1,32,2240]{3,2,1,0:T(8,128)(2,1)S(1)} %collective-permute-done), kind=kLoop, calls=%fused_computation | loop fusion | flops 860160 | bytes 1720320 | tf_op jit(solution)/shard_map/concatenate | solution.py:353
  18.2 5.3 %shard_map.92 = (f32[128,2240]{1,0:T(8,128)}, f32[128,2240]{1,0:T(8,128)}, f32[9,2240]{1,0:T(8,128)}) custom-call(bf16[192,2240]{1,0:T(8,128)(2,1)} %bitcast.14, bf16[192,2240]{1,0:T(8,128)(2,1)} %bitcast.13, f32[9,2240]{1,0:T(8,128)} %reshape.50.refs_2_), custom_call_target="tpu_custom_call" | custom-call | flops 6000000000 | bytes 18000000 | tf_op jit(solution)/shard_map/pallas_call | solution.py:25
  23.4 1.1 %collective-permute-start.4 = (f32[9,2240]{1,0:T(8,128)}, f32[9,2240]{1,0:T(8,128)S(1)}, u32[]{:S(2)}, u32[]{:S(2)}) collective-permute-start(f32[9,2240]{1,0:T(8,128)} %get-tuple-element.20), channel_id=1, source_target_pairs={{0,1},{1,0},{2,3},{3,2},{4,5},{5,4},{6,7},{7,6},{8,9},{9,8},{10,11... | collective-permute-start | bytes 241928 | tf_op jit(solution)/shard_map/ppermute | solution.py:378
  24.6 17.8 %shard_map.94.state_ref = bf16[20,128,128]{2,1,0:T(8,128)(2,1)} custom-call(bf16[20,128,128]{2,1,0:T(8,128)(2,1)} %shard_map.93.local_ref), custom_call_target="tpu_custom_call" | custom-call | flops 24999999488 | bytes 75000000 | tf_op jit(solution)/shard_map/pallas_call | solution.py:359
  42.3 0.0 collective-permute-done.4
  42.4 0.6 collective-permute-start.5
  42.9 13.9 %shard_map.95 = (bf16[128,2240]{1,0:T(8,128)(2,1)}, bf16[128,2240]{1,0:T(8,128)(2,1)}, bf16[20,112,128]{2,1,0:T(8,128)(2,1)}) custom-call(bf16[128,2240]{1,0:T(8,128)(2,1)} %bitcast.15, bf16[128,2240]{1,0:T(8,128)(2,1)} %bitcast.10, f32[128,2240]{1,0:T(8,128)} %get-tuple-element.13.local_ref, bf16[20,128,128]{2,1,0:T(8,128)(2,1)} %shard_map.94.state_ref), custom_call_target="tpu_custom_call" | custom-call | flops 6000000000 | bytes 18000000 | tf_op jit(solution)/shard_map/pallas_call | solution.py:25
  56.9 0.0 collective-permute-done.5
  56.9 4.3 %collective-permute-start.6 = (f32[9,2240]{1,0:T(8,128)S(1)}, f32[9,2240]{1,0:T(8,128)S(1)}, u32[]{:S(2)}, u32[]{:S(2)}) collective-permute-start(f32[9,2240]{1,0:T(8,128)S(1)} %add.13), channel_id=1, source_target_pairs={{0,4},{2,6},{4,0},{6,2},{8,12},{10,14},{12,8},{14,10},{1,5},{3,7},... | collective-permute-start | bytes 241928 | tf_op jit(solution)/shard_map/ppermute | solution.py:378
  61.2 29.0 %shard_map.96.state_ref = bf16[20,112,128]{2,1,0:T(8,128)(2,1)} custom-call(bf16[20,112,128]{2,1,0:T(8,128)(2,1)} %get-tuple-element.17.local_ref), custom_call_target="tpu_custom_call" | custom-call | flops 24999999488 | bytes 75000000 | tf_op jit(solution)/shard_map/pallas_call | solution.py:359
  90.2 0.0 collective-permute-done.6
  90.2 0.1 collective-permute-start.7
  90.3 7.2 %shard_map.97 = (bf16[128,2240]{1,0:T(8,128)(2,1)}, bf16[128,2240]{1,0:T(8,128)(2,1)}) custom-call(bf16[128,2240]{1,0:T(8,128)(2,1)} %bitcast.17, bf16[128,2240]{1,0:T(8,128)(2,1)} %bitcast.12, f32[128,2240]{1,0:T(8,128)} %get-tuple-element.16.conv_ref, bf16[20,112,128]{2,1,0:T(8,128)(2,1)} %shard_map.96.state_ref), custom_call_target="tpu_custom_call" | custom-call | flops 6000000000 | bytes 18000000 | tf_op jit(solution)/shard_map/pallas_call | solution.py:25
  97.6 0.5 collective-permute-done.7
  98.1 0.7 reshape.57
  (8 shorter events, 0.1 us)
Async XLA Ops:
  1.6 15.5 %collective-permute-start = (bf16[1,1,32,2240]{3,2,1,0:T(8,128)(2,1)S(1)}, bf16[1,1,32,2240]{3,2,1,0:T(8,128)(2,1)S(1)}, u32[]{:S(2)}, u32[]{:S(2)}) collective-permute-start(bf16[1,1,32,2240]{3,2,1,0:T(8,128)(2,1)S(1)} %get-tuple-element.23), channel_id=1, source_target_pairs={{0,1},{2,3},{4,5},{6,7},{8,9},{10,11},{12,13},{14,15},{16,17},{18,... | collective-permute-start | bytes 430088 | tf_op jit(solution)/shard_map/ppermute | solution.py:351
  4.1 13.1 %collective-permute-start.1 = (bf16[1,1,32,2240]{3,2,1,0:T(8,128)(2,1)S(1)}, bf16[1,1,32,2240]{3,2,1,0:T(8,128)(2,1)S(1)}, u32[]{:S(2)}, u32[]{:S(2)}) collective-permute-start(bf16[1,1,32,2240]{3,2,1,0:T(8,128)(2,1)S(1)} %get-tuple-element.24), channel_id=1, source_target_pairs={{1,0},{3,2},{5,4},{7,6},{9,8},{11,10},{13,12},{15,14},{17,16},{19,... | collective-permute-start | bytes 430088 | tf_op jit(solution)/shard_map/ppermute | solution.py:352
  6.4 9.7 %collective-permute-start.2 = (bf16[1,1,32,2240]{3,2,1,0:T(8,128)(2,1)S(1)}, bf16[1,1,32,2240]{3,2,1,0:T(8,128)(2,1)S(1)}, u32[]{:S(2)}, u32[]{:S(2)}) collective-permute-start(bf16[1,1,32,2240]{3,2,1,0:T(8,128)(2,1)S(1)} %get-tuple-element.21), channel_id=1, source_target_pairs={{0,1},{2,3},{4,5},{6,7},{8,9},{10,11},{12,13},{14,15},{16,17},{18,... | collective-permute-start | bytes 430088 | tf_op jit(solution)/shard_map/ppermute | solution.py:351
  9.4 6.6 %collective-permute-start.3 = (bf16[1,1,32,2240]{3,2,1,0:T(8,128)(2,1)S(1)}, bf16[1,1,32,2240]{3,2,1,0:T(8,128)(2,1)S(1)}, u32[]{:S(2)}, u32[]{:S(2)}) collective-permute-start(bf16[1,1,32,2240]{3,2,1,0:T(8,128)(2,1)S(1)} %get-tuple-element.22), channel_id=1, source_target_pairs={{1,0},{3,2},{5,4},{7,6},{9,8},{11,10},{13,12},{15,14},{17,16},{19,... | collective-permute-start | bytes 430088 | tf_op jit(solution)/shard_map/ppermute | solution.py:352
  10.7 4.6 %copy-start.3 = (f32[3,3,2240]{2,1,0:T(4,128)S(1)}, f32[3,3,2240]{2,1,0:T(4,128)}, u32[]{:S(2)}) copy-start(f32[3,3,2240]{2,1,0:T(4,128)} %param.9) | copy-start | bytes 241924
  10.7 5.3 %copy-start = (bf16[1,4,32,2240]{3,2,1,0:T(8,128)(2,1)S(1)}, bf16[1,4,32,2240]{3,2,1,0:T(8,128)(2,1)}, u32[]{:S(2)}) copy-start(bf16[1,4,32,2240]{3,2,1,0:T(8,128)(2,1)} %param.8) | copy-start | bytes 1720324
  15.3 1.8 %copy-start.1 = (bf16[1,4,32,2240]{3,2,1,0:T(8,128)(2,1)S(1)}, bf16[1,4,32,2240]{3,2,1,0:T(8,128)(2,1)}, u32[]{:S(2)}) copy-start(bf16[1,4,32,2240]{3,2,1,0:T(8,128)(2,1)} %param.7) | copy-start | bytes 1720324
  23.4 18.9 %copy-start.2 = (f32[9,2240]{1,0:T(8,128)S(1)}, f32[9,2240]{1,0:T(8,128)}, u32[]{:S(2)}) copy-start(f32[9,2240]{1,0:T(8,128)} %get-tuple-element.20) | copy-start | bytes 241924
  23.4 18.9 %collective-permute-start.4 = (f32[9,2240]{1,0:T(8,128)}, f32[9,2240]{1,0:T(8,128)S(1)}, u32[]{:S(2)}, u32[]{:S(2)}) collective-permute-start(f32[9,2240]{1,0:T(8,128)} %get-tuple-element.20), channel_id=1, source_target_pairs={{0,1},{1,0},{2,3},{3,2},{4,5},{5,4},{6,7},{7,6},{8,9},{9,8},{10,11... | collective-permute-start | bytes 241928 | tf_op jit(solution)/shard_map/ppermute | solution.py:378
  42.4 14.5 %collective-permute-start.5 = (f32[9,2240]{1,0:T(8,128)S(1)}, f32[9,2240]{1,0:T(8,128)S(1)}, u32[]{:S(2)}, u32[]{:S(2)}) collective-permute-start(f32[9,2240]{1,0:T(8,128)S(1)} %add.12), channel_id=1, source_target_pairs={{0,2},{2,0},{4,6},{6,4},{8,10},{10,8},{12,14},{14,12},{1,3},{3,1},... | collective-permute-start | bytes 241928 | tf_op jit(solution)/shard_map/ppermute | solution.py:378
  56.9 33.3 %collective-permute-start.6 = (f32[9,2240]{1,0:T(8,128)S(1)}, f32[9,2240]{1,0:T(8,128)S(1)}, u32[]{:S(2)}, u32[]{:S(2)}) collective-permute-start(f32[9,2240]{1,0:T(8,128)S(1)} %add.13), channel_id=1, source_target_pairs={{0,4},{2,6},{4,0},{6,2},{8,12},{10,14},{12,8},{14,10},{1,5},{3,7},... | collective-permute-start | bytes 241928 | tf_op jit(solution)/shard_map/ppermute | solution.py:378
  90.2 7.8 %collective-permute-start.7 = (f32[9,2240]{1,0:T(8,128)S(1)}, f32[9,2240]{1,0:T(8,128)S(1)}, u32[]{:S(2)}, u32[]{:S(2)}) collective-permute-start(f32[9,2240]{1,0:T(8,128)S(1)} %add.14), channel_id=1, source_target_pairs={{0,8},{2,10},{4,12},{6,14},{8,0},{10,2},{12,4},{14,6},{1,9},{3,11}... | collective-permute-start | bytes 241928 | tf_op jit(solution)/shard_map/ppermute | solution.py:378

commit v4 on v3

--- a/solution.py
+++ b/solution.py
@@ -45,13 +45,26 @@
     return high, x - high
 
 
-def conv_body(rows, cols, value_ref, grad_ref, taps_ref, local_ref, conv_ref, taps_grad_ref):
+def conv_body(rows, cols, value_ref, grad_ref, edge_ref, taps_ref, local_ref, conv_ref, taps_grad_ref):
     width = value_ref.shape[1]
     count = rows * cols
+    core = lax.axis_index("space")
     for low in range(0, width, LANES):
         lanes = slice(low, min(low + LANES, width))
-        value = value_ref[:, lanes].astype(F32)
-        grad = grad_ref[:, lanes].astype(F32)
+
+        def banded(ref, which):
+            edge = edge_ref[which, :, lanes].astype(F32)
+            return jnp.concatenate(
+                [
+                    jnp.where(core == 1, edge, 0.0),
+                    ref[:, lanes].astype(F32),
+                    jnp.where(core == 0, edge, 0.0),
+                ],
+                axis=0,
+            )
+
+        value = banded(value_ref, 0)
+        grad = banded(grad_ref, 1)
         col = lax.broadcasted_iota(jnp.int32, value.shape, 0) % cols
         total = value.shape[0]
 
@@ -158,6 +171,7 @@
     local_ref,
     out_ref,
     half_ref,
+    both_ref,
     core_recv,
     pair_send,
     pair_recv,
@@ -226,10 +240,6 @@
     def _():
         greet({"tm": behind})
 
-    @pl.when(order == 0)
-    def _():
-        chain_recv[...] = jnp.zeros_like(chain_recv)
-
     peers = 2 + jnp.minimum(order, 1) + jnp.minimum(links - 1 - order, 1)
     pl.semaphore_wait(barrier, peers)
 
@@ -251,28 +261,46 @@
 
     lax.fori_loop(0, heads, over_cores, 0)
 
+    def give(head, total):
+        out_ref[core * heads + head] = total.astype(BF16)
+        out_copy(head).start()
+
     def over_pairs(head, _):
         pair_copy(head).wait_recv()
         half = half_ref[head]
         both = merge(half, pair_recv[head].astype(F32), lane, extra)
-
-        @pl.when(order > 0)
+        both_ref[head] = both
+
+        @pl.when(order == 0)
         def _():
+            @pl.when(order < links - 1)
+            def _():
+                chain_send[head] = both.astype(BF16)
+                chain_copy(head).start()
+
+            give(head, jnp.where(sums_both, both, half))
+
+        return 0
+
+    lax.fori_loop(0, heads, over_pairs, 0)
+
+    @pl.when(order > 0)
+    def _():
+        def over_chain(head, _):
+            both = both_ref[head]
             chain_copy(head).wait_recv()
-
-        before = chain_recv[head].astype(F32)
-
-        @pl.when(order < links - 1)
-        def _():
-            chain_send[head] = merge(before, both, lane, extra).astype(BF16)
-            chain_copy(head).start()
-
-        mine = jnp.where(sums_both, both, half)
-        out_ref[core * heads + head] = merge(before, mine, lane, extra).astype(BF16)
-        out_copy(head).start()
-        return 0
-
-    lax.fori_loop(0, heads, over_pairs, 0)
+            before = chain_recv[head].astype(F32)
+
+            @pl.when(order < links - 1)
+            def _():
+                chain_send[head] = merge(before, both, lane, extra).astype(BF16)
+                chain_copy(head).start()
+
+            mine = jnp.where(sums_both, both, half_ref[head])
+            give(head, merge(before, mine, lane, extra))
+            return 0
+
+        lax.fori_loop(0, heads, over_chain, 0)
 
     def finish(head, _):
         core_copy(head).wait_send()
@@ -344,13 +372,13 @@
         value_grad_ref[:, lanes] = (mixed[:, :size] + conv_ref[:, lanes]).astype(BF16)
 
 
-def with_edges(block):
-    count = lax.axis_size("space")
-    forward = [(i, i + 1) for i in range(count - 1)]
-    backward = [(i + 1, i) for i in range(count - 1)]
-    low = lax.ppermute(block[:, -1:], "space", forward)
-    high = lax.ppermute(block[:, :1], "space", backward)
-    return jnp.concatenate([low, block, high], axis=1)
+def edge_rows(*blocks):
+    place = lax.axis_index("space")
+    last = blocks[0].shape[1] - 1
+    own = jnp.stack(
+        [lax.dynamic_index_in_dim(a[0], (1 - place) * last, 0, False) for a in blocks]
+    )
+    return lax.ppermute(own, "space", [(0, 1), (1, 0)])
 
 
 def scan_over(local, merge, reverse):
@@ -361,7 +389,7 @@
         out_shape=struct(local.shape, BF16),
         in_specs=[pl.BlockSpec(memory_space=pltpu.VMEM)],
         out_specs=pl.BlockSpec(memory_space=pltpu.VMEM),
-        scratch_shapes=[pltpu.VMEM(half, F32)] + [pltpu.VMEM(half, BF16)] * 5 + [sems] * 4,
+        scratch_shapes=[pltpu.VMEM(half, F32)] * 2 + [pltpu.VMEM(half, BF16)] * 5 + [sems] * 4,
         compiler_params=pltpu.CompilerParams(
             collective_id=int(reverse), has_side_effects=True, vmem_limit_bytes=VMEM_LIMIT
         ),
@@ -390,13 +418,13 @@
         a.reshape(flat) for a in (query_pre, key_pre, value_pre, grad_out)
     )
     partial = call(partial_body, struct((HEADS, LANES, LANES), BF16), key, value)
-    value_rows = with_edges(value_pre).reshape((rows + 2) * cols, width)
-    grad_rows = with_edges(grad_out).reshape((rows + 2) * cols, width)
+    edges = edge_rows(value_pre, grad_out)
     local, conv, taps_grad = call(
         lambda *refs: conv_body(rows, cols, *refs),
         (struct(flat, F32), struct(flat, F32), struct((9, width), F32)),
-        value_rows,
-        grad_rows,
+        value,
+        grad,
+        edges,
         conv_taps.reshape(9, width),
     )
     for axis in ("space", "tm"):

time: 99.2 us -> 94.1 us (0.949)
  starting transfers between devices: 14.1 us -> 9.06 us
  Pallas kernels: 77.8 us -> 80.3 us
  other arithmetic: 2.16 us -> 0.1 us
    ppermute x4 -> x1, starting transfers between devices: 8.03 us -> 0.56 us  [edge_rows(): return lax.ppermute(own, 'space', [(0, 1), (1, 0)])]
    pallas_call x2, Pallas kernels: 46.8 us -> 49.4 us  [scan_over(): pl.pallas_call(functools.partial(scan_body, merge, reverse), out_shape=st...]
    ppermute x4, starting transfers between devices: 6.08 us -> 8.5 us  [summed_over(): x = x + lax.ppermute(x, axis, [(i, i ^ step) for i in range(count)])]
    concatenate x2 -> x0, other arithmetic: 2.09 us -> none  [with_edges(): return jnp.concatenate([low, block, high], axis=1)]
    slice x2 -> x0, local copies, waits for them, and re-layouts: 2.01 us -> none  [with_edges(): low = lax.ppermute(block[:, -1:], 'space', forward)]
    dynamic_slice x0 -> x1, local copies, waits for them, and re-layouts: none -> 1.04 us  [edge_rows(): lax.dynamic_index_in_dim(a[0], (1 - place) * last, 0, False)]
  transfers between devices with their start and end apart: 8 -> 5, of which waited for: 1 -> 1; matrix products, arithmetic and copies ran while one was open for 3% -> 1% of each run, Pallas kernels for 73% -> 80%
where the time goes in v4:
time: 94.1 us; the launch traced here: 93.8 us
  Pallas kernels  80.3 us (85%)
  starting transfers between devices  9.06 us (10%)
  local copies, waits for them, and re-layouts  3.15 us (3%)
    pallas_call x2, Pallas kernels, scan_over(): pl.pallas_call(functools.partial(scan_body, merge, reverse), out_shape=st...  49.4 us
    pallas_call x4, Pallas kernels, call(): pl.pallas_call(body, out_shape=out_shape, in_specs=[pl.BlockSpec(memory_s...  30.9 us
    ppermute x4, starting transfers between devices, summed_over(): x = x + lax.ppermute(x, axis, [(i, i ^ step) for i in range(count)])  8.5 us
  transfers between devices with their start and end apart: 5, of which 1 were waited for; matrix products, arithmetic and copies ran while one was open for 1% of the time, Pallas kernels for 80%

profile of v4, /device:TPU:0, one launch (start us, length us, event | category | flops | bytes accessed | tf_op | source)
XLA Modules:
  0.0 93.8 jit_solution(14953942000083054109)
XLA Ops:
  0.6 0.0 copy-start.1
  0.6 1.0 %dynamic-slice_bitcast_fusion = (bf16[1,32,2240]{2,1,0:T(8,128)(2,1)S(1)}, bf16[1,32,2240]{2,1,0:T(8,128)(2,1)S(1)}) fusion(bf16[1,4,32,2240]{3,2,1,0:T(8,128)(2,1)} %param.8, s32[]{:T(128)S(6)} %select_n.5, bf16[1,4,32,2240]{3,2,1,0:T(8,128)(2,1)} %param.7), kind=kLoop, calls=%fused_computation.1 | loop fusion | bytes 573444 | tf_op jit(solution)/shard_map/jit(dynamic_index_in_dim)/dynamic_slice | solution.py:379
  1.7 0.6 collective-permute-start
  2.3 0.0 copy-done.1
  2.3 0.7 reshape.45.refs_3_
  3.0 4.5 %shard_map.93.local_ref = bf16[20,128,128]{2,1,0:T(8,128)(2,1)} custom-call(bf16[128,2240]{1,0:T(8,128)(2,1)} %bitcast.18, bf16[128,2240]{1,0:T(8,128)(2,1)} %bitcast.14), custom_call_target="tpu_custom_call" | custom-call | flops 6000000000 | bytes 18000000 | tf_op jit(solution)/shard_map/pallas_call | solution.py:25
  7.5 0.0 collective-permute-done.refs_2_
  7.5 0.0 copy-start.2
  7.5 0.7 copy-done.2
  8.2 5.2 %shard_map.92 = (f32[128,2240]{1,0:T(8,128)}, f32[128,2240]{1,0:T(8,128)}, f32[9,2240]{1,0:T(8,128)}) custom-call(bf16[128,2240]{1,0:T(8,128)(2,1)} %bitcast.15, bf16[128,2240]{1,0:T(8,128)(2,1)} %bitcast.12, bf16[2,32,2240]{2,1,0:T(8,128)(2,1)} %copy-done.2, f32[9,2240]{1,0:T(8,128)} %reshape.45.refs_3_), custom_call_target="tpu_custom_call" | custom-call | flops 6000000000 | bytes 18000000 | tf_op jit(solution)/shard_map/pallas_call | solution.py:25
  13.5 0.0 copy-start
  13.5 0.0 collective-permute-start.1
  13.5 18.2 %shard_map.94.state_ref = bf16[20,128,128]{2,1,0:T(8,128)(2,1)} custom-call(bf16[20,128,128]{2,1,0:T(8,128)(2,1)} %shard_map.93.local_ref), custom_call_target="tpu_custom_call" | custom-call | flops 24999999488 | bytes 75000000 | tf_op jit(solution)/shard_map/pallas_call | solution.py:387
  31.8 0.0 collective-permute-done.1
  31.8 0.0 copy-done
  31.8 0.6 collective-permute-start.2
  32.4 13.9 %shard_map.95 = (bf16[128,2240]{1,0:T(8,128)(2,1)}, bf16[128,2240]{1,0:T(8,128)(2,1)}, bf16[20,112,128]{2,1,0:T(8,128)(2,1)}) custom-call(bf16[128,2240]{1,0:T(8,128)(2,1)} %bitcast.17, bf16[128,2240]{1,0:T(8,128)(2,1)} %bitcast.13, f32[128,2240]{1,0:T(8,128)} %get-tuple-element.13.local_ref, bf16[20,128,128]{2,1,0:T(8,128)(2,1)} %shard_map.94.state_ref), custom_call_target="tpu_custom_call" | custom-call | flops 6000000000 | bytes 18000000 | tf_op jit(solution)/shard_map/pallas_call | solution.py:25
  46.3 0.0 collective-permute-done.2
  46.3 7.8 %collective-permute-start.3 = (f32[9,2240]{1,0:T(8,128)S(1)}, f32[9,2240]{1,0:T(8,128)S(1)}, u32[]{:S(2)}, u32[]{:S(2)}) collective-permute-start(f32[9,2240]{1,0:T(8,128)S(1)} %add.19), channel_id=1, source_target_pairs={{0,4},{2,6},{4,0},{6,2},{8,12},{10,14},{12,8},{14,10},{1,5},{3,7},... | collective-permute-start | bytes 241928 | tf_op jit(solution)/shard_map/ppermute | solution.py:406
  54.2 31.1 %shard_map.96.state_ref = bf16[20,112,128]{2,1,0:T(8,128)(2,1)} custom-call(bf16[20,112,128]{2,1,0:T(8,128)(2,1)} %get-tuple-element.17.local_ref), custom_call_target="tpu_custom_call" | custom-call | flops 24999999488 | bytes 75000000 | tf_op jit(solution)/shard_map/pallas_call | solution.py:387
  85.3 0.0 collective-permute-done.3
  85.3 0.1 collective-permute-start.4
  85.4 7.2 %shard_map.97 = (bf16[128,2240]{1,0:T(8,128)(2,1)}, bf16[128,2240]{1,0:T(8,128)(2,1)}) custom-call(bf16[128,2240]{1,0:T(8,128)(2,1)} %bitcast.19, bf16[128,2240]{1,0:T(8,128)(2,1)} %bitcast.16, f32[128,2240]{1,0:T(8,128)} %get-tuple-element.16.conv_ref, bf16[20,112,128]{2,1,0:T(8,128)(2,1)} %shard_map.96.state_ref), custom_call_target="tpu_custom_call" | custom-call | flops 6000000000 | bytes 18000000 | tf_op jit(solution)/shard_map/pallas_call | solution.py:25
  92.6 0.5 collective-permute-done.4
  93.1 0.7 reshape.51
  (5 shorter events, 0.1 us)
Async XLA Ops:
  0.6 1.7 %copy-start.1 = (f32[3,3,2240]{2,1,0:T(4,128)S(1)}, f32[3,3,2240]{2,1,0:T(4,128)}, u32[]{:S(2)}) copy-start(f32[3,3,2240]{2,1,0:T(4,128)} %param.9) | copy-start | bytes 241924
  1.7 5.8 %collective-permute-start = (bf16[2,32,2240]{2,1,0:T(8,128)(2,1)S(1)}, bf16[2,32,2240]{2,1,0:T(8,128)(2,1)S(1)}, u32[]{:S(2)}, u32[]{:S(2)}) collective-permute-start(bf16[2,32,2240]{2,1,0:T(8,128)(2,1)S(1)} %pad_maximum_fusion), channel_id=1, source_target_pairs={{0,1},{1,0},{2,3},{3,2},{4,5},{5,4},{6,7},{7,6},{8,9},{9,8},{10,11... | collective-permute-start | bytes 860168 | tf_op jit(solution)/shard_map/ppermute | solution.py:381
  7.5 0.7 copy-start.2
  13.5 18.3 %copy-start = (f32[9,2240]{1,0:T(8,128)S(1)}, f32[9,2240]{1,0:T(8,128)}, u32[]{:S(2)}) copy-start(f32[9,2240]{1,0:T(8,128)} %get-tuple-element.20) | copy-start | bytes 241924
  13.5 18.3 %collective-permute-start.1 = (f32[9,2240]{1,0:T(8,128)}, f32[9,2240]{1,0:T(8,128)S(1)}, u32[]{:S(2)}, u32[]{:S(2)}) collective-permute-start(f32[9,2240]{1,0:T(8,128)} %get-tuple-element.20), channel_id=1, source_target_pairs={{0,1},{1,0},{2,3},{3,2},{4,5},{5,4},{6,7},{7,6},{8,9},{9,8},{10,11... | collective-permute-start | bytes 241928 | tf_op jit(solution)/shard_map/ppermute | solution.py:406
  31.8 14.5 %collective-permute-start.2 = (f32[9,2240]{1,0:T(8,128)S(1)}, f32[9,2240]{1,0:T(8,128)S(1)}, u32[]{:S(2)}, u32[]{:S(2)}) collective-permute-start(f32[9,2240]{1,0:T(8,128)S(1)} %add.18), channel_id=1, source_target_pairs={{0,2},{2,0},{4,6},{6,4},{8,10},{10,8},{12,14},{14,12},{1,3},{3,1},... | collective-permute-start | bytes 241928 | tf_op jit(solution)/shard_map/ppermute | solution.py:406
  46.3 39.0 %collective-permute-start.3 = (f32[9,2240]{1,0:T(8,128)S(1)}, f32[9,2240]{1,0:T(8,128)S(1)}, u32[]{:S(2)}, u32[]{:S(2)}) collective-permute-start(f32[9,2240]{1,0:T(8,128)S(1)} %add.19), channel_id=1, source_target_pairs={{0,4},{2,6},{4,0},{6,2},{8,12},{10,14},{12,8},{14,10},{1,5},{3,7},... | collective-permute-start | bytes 241928 | tf_op jit(solution)/shard_map/ppermute | solution.py:406
  85.3 7.8 %collective-permute-start.4 = (f32[9,2240]{1,0:T(8,128)S(1)}, f32[9,2240]{1,0:T(8,128)S(1)}, u32[]{:S(2)}, u32[]{:S(2)}) collective-permute-start(f32[9,2240]{1,0:T(8,128)S(1)} %add.20), channel_id=1, source_target_pairs={{0,8},{2,10},{4,12},{6,14},{8,0},{10,2},{12,4},{14,6},{1,9},{3,11}... | collective-permute-start | bytes 241928 | tf_op jit(solution)/shard_map/ppermute | solution.py:406

commit v5 on v4

--- a/solution.py
+++ b/solution.py
@@ -249,40 +249,60 @@
 
     lax.fori_loop(0, heads, begin, 0)
 
-    def over_cores(head, _):
-        core_copy(head).wait_recv()
-        half = merge(
-            local_ref[core * heads + head].astype(F32), core_recv[head].astype(F32), lane, extra
-        )
-        half_ref[head] = half
-        pair_send[head] = half.astype(BF16)
-        pair_copy(head).start()
+    group = 2 if heads % 2 == 0 else 1
+
+    def over_cores(turn, _):
+        batch = [turn * group + i for i in range(group)]
+        for head in batch:
+            core_copy(head).wait_recv()
+        halves = [
+            merge(
+                local_ref[core * heads + head].astype(F32),
+                core_recv[head].astype(F32),
+                lane,
+                extra,
+            )
+            for head in batch
+        ]
+        for head, half in zip(batch, halves):
+            half_ref[head] = half
+            pair_send[head] = half.astype(BF16)
+        for head in batch:
+            pair_copy(head).start()
         return 0
 
-    lax.fori_loop(0, heads, over_cores, 0)
+    lax.fori_loop(0, heads // group, over_cores, 0)
 
     def give(head, total):
         out_ref[core * heads + head] = total.astype(BF16)
         out_copy(head).start()
 
-    def over_pairs(head, _):
-        pair_copy(head).wait_recv()
-        half = half_ref[head]
-        both = merge(half, pair_recv[head].astype(F32), lane, extra)
-        both_ref[head] = both
+    def over_pairs(turn, _):
+        batch = [turn * group + i for i in range(group)]
+        for head in batch:
+            pair_copy(head).wait_recv()
+        halves = [half_ref[head] for head in batch]
+        boths = [
+            merge(half, pair_recv[head].astype(F32), lane, extra)
+            for head, half in zip(batch, halves)
+        ]
+        for head, both in zip(batch, boths):
+            both_ref[head] = both
 
         @pl.when(order == 0)
         def _():
             @pl.when(order < links - 1)
             def _():
-                chain_send[head] = both.astype(BF16)
-                chain_copy(head).start()
-
-            give(head, jnp.where(sums_both, both, half))
+                for head, both in zip(batch, boths):
+                    chain_send[head] = both.astype(BF16)
+                    chain_copy(head).start()
+
+            for head, half, both in zip(batch, halves, boths):
+                give(head, jnp.where(sums_both, both, half))
 
         return 0
 
-    lax.fori_loop(0, heads, over_pairs, 0)
+    lax.fori_loop(0, heads // group, over_pairs, 0)
 
     @pl.when(order > 0)
     def _():

time: 94.1 us -> 94.6 us (level)
  no operation moved by 1% of the time
where the time goes in v5:
time: 94.6 us; the launch traced here: 94.3 us
  Pallas kernels  81.1 us (86%)
  starting transfers between devices  8.71 us (9%)
  local copies, waits for them, and re-layouts  3.15 us (3%)
    pallas_call x2, Pallas kernels, scan_over(): pl.pallas_call(functools.partial(scan_body, merge, reverse), out_shape=st...  50.1 us
    pallas_call x4, Pallas kernels, call(): pl.pallas_call(body, out_shape=out_shape, in_specs=[pl.BlockSpec(memory_s...  30.9 us
    ppermute x4, starting transfers between devices, summed_over(): x = x + lax.ppermute(x, axis, [(i, i ^ step) for i in range(count)])  8.15 us
  transfers between devices with their start and end apart: 5, of which 1 were waited for; matrix products, arithmetic and copies ran while one was open for 1% of the time, Pallas kernels for 80%

profile of v5, /device:TPU:0, one launch (start us, length us, event | category | flops | bytes accessed | tf_op | source)
XLA Modules:
  0.0 94.3 jit_solution(3412314992980936324)
XLA Ops:
  0.6 0.0 copy-start.1
  0.6 1.0 %dynamic-slice_bitcast_fusion = (bf16[1,32,2240]{2,1,0:T(8,128)(2,1)S(1)}, bf16[1,32,2240]{2,1,0:T(8,128)(2,1)S(1)}) fusion(bf16[1,4,32,2240]{3,2,1,0:T(8,128)(2,1)} %param.8, s32[]{:T(128)S(6)} %select_n.5, bf16[1,4,32,2240]{3,2,1,0:T(8,128)(2,1)} %param.7), kind=kLoop, calls=%fused_computation.1 | loop fusion | bytes 573444 | tf_op jit(solution)/shard_map/jit(dynamic_index_in_dim)/dynamic_slice | solution.py:399
  1.7 0.6 collective-permute-start
  2.3 0.0 copy-done.1
  2.3 0.7 reshape.45.refs_3_
  3.0 4.5 %shard_map.93.local_ref = bf16[20,128,128]{2,1,0:T(8,128)(2,1)} custom-call(bf16[128,2240]{1,0:T(8,128)(2,1)} %bitcast.18, bf16[128,2240]{1,0:T(8,128)(2,1)} %bitcast.14), custom_call_target="tpu_custom_call" | custom-call | flops 6000000000 | bytes 18000000 | tf_op jit(solution)/shard_map/pallas_call | solution.py:25
  7.5 0.0 collective-permute-done.refs_2_
  7.5 0.0 copy-start.2
  7.5 0.7 copy-done.2
  8.2 5.2 %shard_map.92 = (f32[128,2240]{1,0:T(8,128)}, f32[128,2240]{1,0:T(8,128)}, f32[9,2240]{1,0:T(8,128)}) custom-call(bf16[128,2240]{1,0:T(8,128)(2,1)} %bitcast.15, bf16[128,2240]{1,0:T(8,128)(2,1)} %bitcast.12, bf16[2,32,2240]{2,1,0:T(8,128)(2,1)} %copy-done.2, f32[9,2240]{1,0:T(8,128)} %reshape.45.refs_3_), custom_call_target="tpu_custom_call" | custom-call | flops 6000000000 | bytes 18000000 | tf_op jit(solution)/shard_map/pallas_call | solution.py:25
  13.5 0.0 copy-start
  13.5 0.0 collective-permute-start.1
  13.5 18.9 %shard_map.94.state_ref = bf16[20,128,128]{2,1,0:T(8,128)(2,1)} custom-call(bf16[20,128,128]{2,1,0:T(8,128)(2,1)} %shard_map.93.local_ref), custom_call_target="tpu_custom_call" | custom-call | flops 24999999488 | bytes 75000000 | tf_op jit(solution)/shard_map/pallas_call | solution.py:407
  32.4 0.0 collective-permute-done.1
  32.5 0.0 copy-done
  32.5 0.6 collective-permute-start.2
  33.1 13.9 %shard_map.95 = (bf16[128,2240]{1,0:T(8,128)(2,1)}, bf16[128,2240]{1,0:T(8,128)(2,1)}, bf16[20,112,128]{2,1,0:T(8,128)(2,1)}) custom-call(bf16[128,2240]{1,0:T(8,128)(2,1)} %bitcast.17, bf16[128,2240]{1,0:T(8,128)(2,1)} %bitcast.13, f32[128,2240]{1,0:T(8,128)} %get-tuple-element.13.local_ref, bf16[20,128,128]{2,1,0:T(8,128)(2,1)} %shard_map.94.state_ref), custom_call_target="tpu_custom_call" | custom-call | flops 6000000000 | bytes 18000000 | tf_op jit(solution)/shard_map/pallas_call | solution.py:25
  47.0 0.0 collective-permute-done.2
  47.0 7.5 %collective-permute-start.3 = (f32[9,2240]{1,0:T(8,128)S(1)}, f32[9,2240]{1,0:T(8,128)S(1)}, u32[]{:S(2)}, u32[]{:S(2)}) collective-permute-start(f32[9,2240]{1,0:T(8,128)S(1)} %add.19), channel_id=1, source_target_pairs={{0,4},{2,6},{4,0},{6,2},{8,12},{10,14},{12,8},{14,10},{1,5},{3,7},... | collective-permute-start | bytes 241928 | tf_op jit(solution)/shard_map/ppermute | solution.py:426
  54.5 31.2 %shard_map.96.state_ref = bf16[20,112,128]{2,1,0:T(8,128)(2,1)} custom-call(bf16[20,112,128]{2,1,0:T(8,128)(2,1)} %get-tuple-element.17.local_ref), custom_call_target="tpu_custom_call" | custom-call | flops 24999999488 | bytes 75000000 | tf_op jit(solution)/shard_map/pallas_call | solution.py:407
  85.7 0.0 collective-permute-done.3
  85.7 0.1 collective-permute-start.4
  85.8 7.2 %shard_map.97 = (bf16[128,2240]{1,0:T(8,128)(2,1)}, bf16[128,2240]{1,0:T(8,128)(2,1)}) custom-call(bf16[128,2240]{1,0:T(8,128)(2,1)} %bitcast.19, bf16[128,2240]{1,0:T(8,128)(2,1)} %bitcast.16, f32[128,2240]{1,0:T(8,128)} %get-tuple-element.16.conv_ref, bf16[20,112,128]{2,1,0:T(8,128)(2,1)} %shard_map.96.state_ref), custom_call_target="tpu_custom_call" | custom-call | flops 6000000000 | bytes 18000000 | tf_op jit(solution)/shard_map/pallas_call | solution.py:25
  93.1 0.5 collective-permute-done.4
  93.6 0.7 reshape.51
  (5 shorter events, 0.1 us)
Async XLA Ops:
  0.6 1.7 %copy-start.1 = (f32[3,3,2240]{2,1,0:T(4,128)S(1)}, f32[3,3,2240]{2,1,0:T(4,128)}, u32[]{:S(2)}) copy-start(f32[3,3,2240]{2,1,0:T(4,128)} %param.9) | copy-start | bytes 241924
  1.7 5.8 %collective-permute-start = (bf16[2,32,2240]{2,1,0:T(8,128)(2,1)S(1)}, bf16[2,32,2240]{2,1,0:T(8,128)(2,1)S(1)}, u32[]{:S(2)}, u32[]{:S(2)}) collective-permute-start(bf16[2,32,2240]{2,1,0:T(8,128)(2,1)S(1)} %pad_maximum_fusion), channel_id=1, source_target_pairs={{0,1},{1,0},{2,3},{3,2},{4,5},{5,4},{6,7},{7,6},{8,9},{9,8},{10,11... | collective-permute-start | bytes 860168 | tf_op jit(solution)/shard_map/ppermute | solution.py:401
  7.5 0.7 copy-start.2
  13.5 19.0 %copy-start = (f32[9,2240]{1,0:T(8,128)S(1)}, f32[9,2240]{1,0:T(8,128)}, u32[]{:S(2)}) copy-start(f32[9,2240]{1,0:T(8,128)} %get-tuple-element.20) | copy-start | bytes 241924
  13.5 19.0 %collective-permute-start.1 = (f32[9,2240]{1,0:T(8,128)}, f32[9,2240]{1,0:T(8,128)S(1)}, u32[]{:S(2)}, u32[]{:S(2)}) collective-permute-start(f32[9,2240]{1,0:T(8,128)} %get-tuple-element.20), channel_id=1, source_target_pairs={{0,1},{1,0},{2,3},{3,2},{4,5},{5,4},{6,7},{7,6},{8,9},{9,8},{10,11... | collective-permute-start | bytes 241928 | tf_op jit(solution)/shard_map/ppermute | solution.py:426
  32.5 14.5 %collective-permute-start.2 = (f32[9,2240]{1,0:T(8,128)S(1)}, f32[9,2240]{1,0:T(8,128)S(1)}, u32[]{:S(2)}, u32[]{:S(2)}) collective-permute-start(f32[9,2240]{1,0:T(8,128)S(1)} %add.18), channel_id=1, source_target_pairs={{0,2},{2,0},{4,6},{6,4},{8,10},{10,8},{12,14},{14,12},{1,3},{3,1},... | collective-permute-start | bytes 241928 | tf_op jit(solution)/shard_map/ppermute | solution.py:426
  47.0 38.7 %collective-permute-start.3 = (f32[9,2240]{1,0:T(8,128)S(1)}, f32[9,2240]{1,0:T(8,128)S(1)}, u32[]{:S(2)}, u32[]{:S(2)}) collective-permute-start(f32[9,2240]{1,0:T(8,128)S(1)} %add.19), channel_id=1, source_target_pairs={{0,4},{2,6},{4,0},{6,2},{8,12},{10,14},{12,8},{14,10},{1,5},{3,7},... | collective-permute-start | bytes 241928 | tf_op jit(solution)/shard_map/ppermute | solution.py:426
  85.7 7.8 %collective-permute-start.4 = (f32[9,2240]{1,0:T(8,128)S(1)}, f32[9,2240]{1,0:T(8,128)S(1)}, u32[]{:S(2)}, u32[]{:S(2)}) collective-permute-start(f32[9,2240]{1,0:T(8,128)S(1)} %add.20), channel_id=1, source_target_pairs={{0,8},{2,10},{4,12},{6,14},{8,0},{10,2},{12,4},{14,6},{1,9},{3,11}... | collective-permute-start | bytes 241928 | tf_op jit(solution)/shard_map/ppermute | solution.py:426

commit v6 on v4

--- a/solution.py
+++ b/solution.py
@@ -168,8 +168,13 @@
 def scan_body(
     merge,
     reverse,
-    local_ref,
-    out_ref,
+    work,
+    inputs,
+    *refs,
+):
+    local_ref, out_ref = refs[0], refs[1 + inputs]
+    work_refs = refs[1 : 1 + inputs] + refs[2 + inputs : -11]
+    (
     half_ref,
     both_ref,
     core_recv,
@@ -181,7 +186,7 @@
     pair_sems,
     chain_sems,
     out_sems,
-):
+    ) = refs[-11:]
     heads = core_recv.shape[0]
     core = lax.axis_index("space")
     place = lax.axis_index("tm")
@@ -284,6 +289,10 @@
 
     lax.fori_loop(0, heads, over_pairs, 0)
 
+    @pl.when(order == links - 1)
+    def _():
+        work(*work_refs)
+
     @pl.when(order > 0)
     def _():
         def over_chain(head, _):
@@ -301,6 +310,10 @@
             return 0
 
         lax.fori_loop(0, heads, over_chain, 0)
+
+    @pl.when(order < links - 1)
+    def _():
+        work(*work_refs)
 
     def finish(head, _):
         core_copy(head).wait_send()
@@ -381,20 +394,20 @@
     return lax.ppermute(own, "space", [(0, 1), (1, 0)])
 
 
-def scan_over(local, merge, reverse):
+def scan_over(local, merge, reverse, work=lambda: None, args=(), outs=()):
     half = (local.shape[0] // 2,) + local.shape[1:]
     sems = pltpu.SemaphoreType.DMA((2, half[0]))
     return pl.pallas_call(
-        functools.partial(scan_body, merge, reverse),
-        out_shape=struct(local.shape, BF16),
-        in_specs=[pl.BlockSpec(memory_space=pltpu.VMEM)],
-        out_specs=pl.BlockSpec(memory_space=pltpu.VMEM),
+        functools.partial(scan_body, merge, reverse, work, len(args)),
+        out_shape=(struct(local.shape, BF16),) + tuple(outs),
+        in_specs=[pl.BlockSpec(memory_space=pltpu.VMEM)] * (1 + len(args)),
+        out_specs=(pl.BlockSpec(memory_space=pltpu.VMEM),) * (1 + len(outs)),
         scratch_shapes=[pltpu.VMEM(half, F32)] * 2 + [pltpu.VMEM(half, BF16)] * 5 + [sems] * 4,
         compiler_params=pltpu.CompilerParams(
             collective_id=int(reverse), has_side_effects=True, vmem_limit_bytes=VMEM_LIMIT
         ),
         cost_estimate=cost(25),
-    )(local)
+    )(local, *args)
 
 
 def summed_over(x, axis):
@@ -419,18 +432,17 @@
     )
     partial = call(partial_body, struct((HEADS, LANES, LANES), BF16), key, value)
     edges = edge_rows(value_pre, grad_out)
-    local, conv, taps_grad = call(
+    state, local, conv, taps_grad = scan_over(
+        partial,
+        merge_packed,
+        False,
         lambda *refs: conv_body(rows, cols, *refs),
+        (value, grad, edges, conv_taps.reshape(9, width)),
         (struct(flat, F32), struct(flat, F32), struct((9, width), F32)),
-        value,
-        grad,
-        edges,
-        conv_taps.reshape(9, width),
     )
     for axis in ("space", "tm"):
         taps_grad = summed_over(taps_grad, axis)
     taps_grad = taps_grad.reshape(3, 3, width)
-    state = scan_over(partial, merge_packed, False)
     attended, query_grad, grad_partial = call(
         forward_body,
         (struct(flat, BF16), struct(flat, BF16), struct((HEADS, HEAD_DIM, LANES), BF16)),
@@ -439,7 +451,7 @@
         local,
         state,
     )
-    grad_state = scan_over(grad_partial, add_packed, True)
+    (grad_state,) = scan_over(grad_partial, add_packed, True)
     key_grad, value_grad = call(
         backward_body,
         (struct(flat, BF16), struct(flat, BF16)),

time: 94.1 us -> 92.1 us (0.979)
  Pallas kernels: 80.3 us -> 77.6 us
  starting transfers between devices: 9.06 us -> 7.25 us
  waiting for transfers between devices: 0.49 us -> 2.06 us
    pallas_call x4 -> x3, Pallas kernels: 30.9 us -> 25.7 us  [call(): pl.pallas_call(body, out_shape=out_shape, in_specs=[pl.BlockSpec(memory_s...]
    pallas_call x2, Pallas kernels: 49.4 us -> 51.9 us  [scan_over(): pl.pallas_call(functools.partial(scan_body, merge, reverse, work, len(arg...]
    ppermute x4, starting transfers between devices: 8.5 us -> 6.69 us  [summed_over(): x = x + lax.ppermute(x, axis, [(i, i ^ step) for i in range(count)])]
    ppermute x4, waiting for transfers between devices: 0.49 us -> 2.06 us  [summed_over(): x = x + lax.ppermute(x, axis, [(i, i ^ step) for i in range(count)])]
  transfers between devices with their start and end apart: 5 -> 5, of which waited for: 1 -> 2; matrix products, arithmetic and copies ran while one was open for 1% -> 1% of each run, Pallas kernels for 80% -> 62%
where the time goes in v6:
time: 92.1 us; the launch traced here: 91.7 us
  Pallas kernels  77.6 us (84%)
  starting transfers between devices  7.25 us (8%)
  local copies, waits for them, and re-layouts  3.14 us (3%)
  waiting for transfers between devices  2.06 us (2%)
  other arithmetic  1.01 us (1%)
    pallas_call x2, Pallas kernels, scan_over(): pl.pallas_call(functools.partial(scan_body, merge, reverse, work, len(arg...  51.9 us
    pallas_call x3, Pallas kernels, call(): pl.pallas_call(body, out_shape=out_shape, in_specs=[pl.BlockSpec(memory_s...  25.7 us
    ppermute x4, starting transfers between devices, summed_over(): x = x + lax.ppermute(x, axis, [(i, i ^ step) for i in range(count)])  6.69 us
    ppermute x4, waiting for transfers between devices, summed_over(): x = x + lax.ppermute(x, axis, [(i, i ^ step) for i in range(count)])  2.06 us
  transfers between devices with their start and end apart: 5, of which 2 were waited for; matrix products, arithmetic and copies ran while one was open for 1% of the time, Pallas kernels for 62%

profile of v6, /device:TPU:0, one launch (start us, length us, event | category | flops | bytes accessed | tf_op | source)
XLA Modules:
  0.0 91.7 jit_solution(10225447536996455408)
XLA Ops:
  0.6 0.0 copy-start
  0.6 1.0 %dynamic-slice_bitcast_fusion = (bf16[1,32,2240]{2,1,0:T(8,128)(2,1)S(1)}, bf16[1,32,2240]{2,1,0:T(8,128)(2,1)S(1)}) fusion(bf16[1,4,32,2240]{3,2,1,0:T(8,128)(2,1)} %param.8, s32[]{:T(128)S(6)} %select_n.5, bf16[1,4,32,2240]{3,2,1,0:T(8,128)(2,1)} %param.7), kind=kLoop, calls=%fused_computation.1 | loop fusion | bytes 573444 | tf_op jit(solution)/shard_map/jit(dynamic_index_in_dim)/dynamic_slice | solution.py:392
  1.7 0.6 collective-permute-start
  2.3 0.0 copy-done
  2.3 0.7 reshape.46.refs_4_
  3.0 4.5 %shard_map.92.refs_0_ = bf16[20,128,128]{2,1,0:T(8,128)(2,1)} custom-call(bf16[128,2240]{1,0:T(8,128)(2,1)} %bitcast.18, bf16[128,2240]{1,0:T(8,128)(2,1)} %bitcast.14), custom_call_target="tpu_custom_call" | custom-call | flops 6000000000 | bytes 18000000 | tf_op jit(solution)/shard_map/pallas_call | solution.py:25
  7.5 0.0 collective-permute-done.refs_3_
  7.5 0.0 copy-start.1
  7.5 0.7 copy-done.1
  8.2 20.7 %shard_map.93 = (bf16[20,128,128]{2,1,0:T(8,128)(2,1)}, f32[128,2240]{1,0:T(8,128)}, f32[128,2240]{1,0:T(8,128)}, f32[9,2240]{1,0:T(8,128)}) custom-call(bf16[20,128,128]{2,1,0:T(8,128)(2,1)} %shard_map.92.refs_0_, bf16[128,2240]{1,0:T(8,128)(2,1)} %bitcast.15, bf16[128,2240]{1,0:T(8,128)(2,1)} %bitcast.12, bf16[2,32,2240]{2,1,0:T(8,128)(2,1)} %copy-done.1, ...), custom_call_target="tpu_custom_call" | custom-call | flops 24999999488 | bytes 75000000 | tf_op jit(solution)/shard_map/pallas_call | solution.py:400
  28.9 0.1 collective-permute-start.1
  29.0 1.6 %collective-permute-done.1 = f32[9,2240]{1,0:T(8,128)S(1)} collective-permute-done((f32[9,2240]{1,0:T(8,128)}, f32[9,2240]{1,0:T(8,128)S(1)}, u32[]{:S(2)}, u32[]{:S(2)}) %collective-permute-start.1) | collective-permute-done | bytes 80672 | tf_op jit(solution)/shard_map/ppermute | solution.py:419
  30.6 0.9 %add.18 = f32[9,2240]{1,0:T(8,128)S(1)} add(f32[9,2240]{1,0:T(8,128)} %get-tuple-element.22, f32[9,2240]{1,0:T(8,128)S(1)} %collective-permute-done.1) | non-fusion elementwise | flops 20160 | bytes 241920 | tf_op jit(solution)/shard_map/add | solution.py:419
  31.5 0.6 collective-permute-start.2
  32.1 13.9 %shard_map.94 = (bf16[128,2240]{1,0:T(8,128)(2,1)}, bf16[128,2240]{1,0:T(8,128)(2,1)}, bf16[20,112,128]{2,1,0:T(8,128)(2,1)}) custom-call(bf16[128,2240]{1,0:T(8,128)(2,1)} %bitcast.17, bf16[128,2240]{1,0:T(8,128)(2,1)} %bitcast.13, f32[128,2240]{1,0:T(8,128)} %get-tuple-element.14.local_ref, bf16[20,128,128]{2,1,0:T(8,128)(2,1)} %get-tuple-element.15.state_ref), custom_call_target="tpu_custom_call" | custom-call | flops 6000000000 | bytes 18000000 | tf_op jit(solution)/shard_map/pallas_call | solution.py:25
  46.0 0.0 collective-permute-done.2
  46.0 6.0 %collective-permute-start.3 = (f32[9,2240]{1,0:T(8,128)S(1)}, f32[9,2240]{1,0:T(8,128)S(1)}, u32[]{:S(2)}, u32[]{:S(2)}) collective-permute-start(f32[9,2240]{1,0:T(8,128)S(1)} %add.19), channel_id=1, source_target_pairs={{0,4},{2,6},{4,0},{6,2},{8,12},{10,14},{12,8},{14,10},{1,5},{3,7},... | collective-permute-start | bytes 241928 | tf_op jit(solution)/shard_map/ppermute | solution.py:419
  52.0 31.2 %shard_map.95.state_ref = bf16[20,112,128]{2,1,0:T(8,128)(2,1)} custom-call(bf16[20,112,128]{2,1,0:T(8,128)(2,1)} %get-tuple-element.19.refs_0_), custom_call_target="tpu_custom_call" | custom-call | flops 24999999488 | bytes 75000000 | tf_op jit(solution)/shard_map/pallas_call | solution.py:400
  83.2 0.0 collective-permute-done.3
  83.2 0.1 collective-permute-start.4
  83.3 7.2 %shard_map.96 = (bf16[128,2240]{1,0:T(8,128)(2,1)}, bf16[128,2240]{1,0:T(8,128)(2,1)}) custom-call(bf16[128,2240]{1,0:T(8,128)(2,1)} %bitcast.19, bf16[128,2240]{1,0:T(8,128)(2,1)} %bitcast.16, f32[128,2240]{1,0:T(8,128)} %get-tuple-element.18.conv_ref, bf16[20,112,128]{2,1,0:T(8,128)(2,1)} %shard_map.95.state_ref), custom_call_target="tpu_custom_call" | custom-call | flops 6000000000 | bytes 18000000 | tf_op jit(solution)/shard_map/pallas_call | solution.py:25
  90.6 0.5 collective-permute-done.4
  91.1 0.7 reshape.51
  (4 shorter events, 0.1 us)
Async XLA Ops:
  0.6 1.7 %copy-start = (f32[3,3,2240]{2,1,0:T(4,128)S(1)}, f32[3,3,2240]{2,1,0:T(4,128)}, u32[]{:S(2)}) copy-start(f32[3,3,2240]{2,1,0:T(4,128)} %param.9) | copy-start | bytes 241924
  1.7 5.8 %collective-permute-start = (bf16[2,32,2240]{2,1,0:T(8,128)(2,1)S(1)}, bf16[2,32,2240]{2,1,0:T(8,128)(2,1)S(1)}, u32[]{:S(2)}, u32[]{:S(2)}) collective-permute-start(bf16[2,32,2240]{2,1,0:T(8,128)(2,1)S(1)} %pad_maximum_fusion), channel_id=1, source_target_pairs={{0,1},{1,0},{2,3},{3,2},{4,5},{5,4},{6,7},{7,6},{8,9},{9,8},{10,11... | collective-permute-start | bytes 860168 | tf_op jit(solution)/shard_map/ppermute | solution.py:394
  7.5 0.7 copy-start.1
  28.9 1.6 %collective-permute-start.1 = (f32[9,2240]{1,0:T(8,128)}, f32[9,2240]{1,0:T(8,128)S(1)}, u32[]{:S(2)}, u32[]{:S(2)}) collective-permute-start(f32[9,2240]{1,0:T(8,128)} %get-tuple-element.22), channel_id=1, source_target_pairs={{0,1},{1,0},{2,3},{3,2},{4,5},{5,4},{6,7},{7,6},{8,9},{9,8},{10,11... | collective-permute-start | bytes 241928 | tf_op jit(solution)/shard_map/ppermute | solution.py:419
  31.5 14.5 %collective-permute-start.2 = (f32[9,2240]{1,0:T(8,128)S(1)}, f32[9,2240]{1,0:T(8,128)S(1)}, u32[]{:S(2)}, u32[]{:S(2)}) collective-permute-start(f32[9,2240]{1,0:T(8,128)S(1)} %add.18), channel_id=1, source_target_pairs={{0,2},{2,0},{4,6},{6,4},{8,10},{10,8},{12,14},{14,12},{1,3},{3,1},... | collective-permute-start | bytes 241928 | tf_op jit(solution)/shard_map/ppermute | solution.py:419
  46.0 37.2 %collective-permute-start.3 = (f32[9,2240]{1,0:T(8,128)S(1)}, f32[9,2240]{1,0:T(8,128)S(1)}, u32[]{:S(2)}, u32[]{:S(2)}) collective-permute-start(f32[9,2240]{1,0:T(8,128)S(1)} %add.19), channel_id=1, source_target_pairs={{0,4},{2,6},{4,0},{6,2},{8,12},{10,14},{12,8},{14,10},{1,5},{3,7},... | collective-permute-start | bytes 241928 | tf_op jit(solution)/shard_map/ppermute | solution.py:419
  83.2 7.8 %collective-permute-start.4 = (f32[9,2240]{1,0:T(8,128)S(1)}, f32[9,2240]{1,0:T(8,128)S(1)}, u32[]{:S(2)}, u32[]{:S(2)}) collective-permute-start(f32[9,2240]{1,0:T(8,128)S(1)} %add.20), channel_id=1, source_target_pairs={{0,8},{2,10},{4,12},{6,14},{8,0},{10,2},{12,4},{14,6},{1,9},{3,11}... | collective-permute-start | bytes 241928 | tf_op jit(solution)/shard_map/ppermute | solution.py:419
